TPU v7x, 768 devices: a whole 4x8x12 slice. The times are simulated.
768 devices in a mesh: ctx: 192 (over y, z_lo, x, core), head: 4 (over z_hi).
Axes of the slice: x: 4, y: 8, z: 12 (z_hi: 4, z_lo: 3; z = z_hi * 3 + z_lo), core: 2. Of those that a mesh axis runs over, the one named last changes fastest.
Arguments:
- patches: bfloat16 [49152, 2560], P('ctx', 'head'), may hold values from -120 to 120
- merge_index: int32 [192, 2], P('ctx'), may hold values from 0 to 383, as said below
- merge_vals: bfloat16 [192, 2, 128, 128], P('ctx'), may hold values from -0.375 to 0.375
- merger_weight: bfloat16 [2560, 4096], P('head'), may hold values from -0.125 to 0.125
- proj_weight: bfloat16 [4096, 3072], P(None, 'head'), may hold values from -0.09375 to 0.09375
- frame_ids: int32 [24576], replicated, may hold values from 0 to 575, as said below
Outputs:
- attended: bfloat16 [24576, 2048], P('ctx', 'head')
Inputs may be any that keep to these rules, and one draw needn't show every extreme that they name: `merge_index`: the two entries of output block b are two different input blocks out of 2b - 1, 2b and 2b + 1, in rising order; never 2b - 1 when b is the first block of a video; always 2b - 1 when b is the first block of a slab (1 output blocks a slab) that is not the first of a video; the last output block always takes block 2b + 1. `frame_ids`: frame ids never fall along the tokens and frames never cross slabs: every slab of 128 tokens holds 3 frames, the first of 1 to 63 tokens, then frames of 64 tokens, the last one shorter.
All inputs are finite; a program needn't handle non-finite values.
Results may differ from a plain program's by a relative error of at most 0.033.
Values may be sent and summed in bfloat16 or wider, within the bound.
No kernel may reach another device: no remote copies, remote signals or barrier semaphores. Data moves between devices by JAX's collectives and lax.ppermute only.
A program may use at most 128 MiB of HBM per device.

v0:
```python
import math

import jax
import jax.numpy as jnp
from jax import lax
from jax.experimental import pallas as pl
from jax.experimental.pallas import tpu as pltpu
from jax.sharding import PartitionSpec as P


HD = 128
QPK = 4
TOK = 128
QUARTER = 32
HALF = 16
NY, NZ, NX, NC = 8, 3, 4, 2
FIRST_NY = 5
FAR = 4
NEG = -1e30
LOG2E = 1.0 / math.log(2.0)


def split_index(i):
    return i // (NZ * NX * NC), i // (NX * NC) % NZ, i // NC % NX, i % NC


def join_index(y, z, x, c):
    return ((y * NZ + z) * NX + x) * NC + c


def move(shard, target):
    pairs = []
    for i in range(NY * NZ * NX * NC):
        to = target(*split_index(i))
        if to is not None:
            pairs.append((i, join_index(*to)))
    return lax.ppermute(shard, "ctx", pairs)


def along_y(shard, by):
    def target(y, z, x, c):
        to = y + by
        if to >= NY or (to >= FIRST_NY) != (y >= FIRST_NY):
            return None
        return to, z, x, c

    return move(shard, target)


def along_z(shard, by):
    return move(shard, lambda y, z, x, c: (y, (z + by) % NZ, x, c))


def along_x(shard, by):
    return move(shard, lambda y, z, x, c: (y, z, (x + by) % NX, c))


def other_core(shard):
    return move(shard, lambda y, z, x, c: (y, z, x, 1 - c))


def next_slab(shard):
    count = NY * NZ * NX * NC
    first = FIRST_NY * NZ * NX * NC
    return lax.ppermute(shard, "ctx", [(i, i + 1) for i in range(count - 1) if i + 1 != first])


def along_head(shard, by):
    return lax.ppermute(shard, "head", [(i, (i + by) % 4) for i in range(4)])


def rows_of(q):
    return jnp.concatenate([q[:, p * HD : (p + 1) * HD] for p in range(QPK)], axis=0)


def scores_of(q, keys):
    return lax.dot_general(q, keys, (((1,), (1,)), ((), ())), preferred_element_type=jnp.float32)


def with_ones(values):
    return jnp.concatenate([values, jnp.ones(values.shape, values.dtype)], axis=1)


def eye():
    shape = (TOK, TOK)
    return lax.broadcasted_iota(jnp.int32, shape, 0) == lax.broadcasted_iota(jnp.int32, shape, 1)


def as_column(row):
    square = jnp.where(eye(), jnp.broadcast_to(row, (TOK, TOK)), 0.0)
    return jnp.sum(square, axis=1, keepdims=True)


def as_row(square):
    return jnp.sum(jnp.where(eye(), square, 0.0), axis=0, keepdims=True)


def saved(acc, top):
    lane = lax.broadcasted_iota(jnp.int32, (1, HD), 1)
    return jnp.concatenate([acc[:, :HD], jnp.where(lane < HD // 2, acc[:, HD:], top)], axis=1)


def restored(state_ref):
    total = jnp.broadcast_to(state_ref[:, HD : HD + 1], (state_ref.shape[0], HD))
    return jnp.concatenate([state_ref[:, :HD], total], axis=1), state_ref[:, 2 * HD - 1 : 2 * HD]


def weighted(parts, top, acc):
    for s, v in parts:
        w = jnp.exp2(s - top).astype(jnp.bfloat16)
        acc += jnp.dot(w, with_ones(v), preferred_element_type=jnp.float32)
    return acc


def near_kernel(place_ref, q_ref, own_ref, other_ref, frames_ref, state_ref):
    earlier, x, c = place_ref[0], place_ref[2], place_ref[3]
    q = rows_of(q_ref[0])
    mine = frames_ref[pl.ds(lax.rem(x + NX - pl.program_id(0), NX) * NC + c, 1), :]
    column = as_column(mine.astype(jnp.float32))
    column = jnp.concatenate([column] * QPK, axis=0)
    parts = []
    for ref, row in ((own_ref, x * NC + c), (other_ref, x * NC + 1 - c)):
        frame = frames_ref[pl.ds(row, 1), :].astype(jnp.float32)
        s = scores_of(q, ref[:TOK, :HD])
        parts.append((jnp.where(frame <= column, s, NEG), ref[:TOK, HD:]))
    lane = lax.broadcasted_iota(jnp.int32, (1, FAR * TOK), 1)
    bias = jnp.where(lane < earlier * TOK, 0.0, NEG)
    for ref in (own_ref, other_ref):
        parts.append((scores_of(q, ref[TOK:, :HD]) + bias, ref[TOK:, HD:]))
    top = jnp.full((ROWS, 1), NEG, jnp.float32)
    for s, _ in parts:
        top = jnp.maximum(top, jnp.max(s, axis=1, keepdims=True))
    acc = weighted(parts, top, jnp.zeros((ROWS, 2 * HD), jnp.float32))
    state_ref[...] = saved(acc, top)


def far_sum(place_ref, q_ref, sides_ref, state_ref):
    earlier, z = place_ref[0], place_ref[1]
    q = rows_of(q_ref[0])
    half = (FAR + 1) * TOK
    acc, old = restored(state_ref)
    lane = lax.broadcasted_iota(jnp.int32, (1, half), 1)
    parts = []
    top = old
    for b in range(2):
        low = jnp.where(z >= b + 1, 0, TOK)
        bias = jnp.where((lane >= low) & (lane < (earlier + 1) * TOK), 0.0, NEG)
        s = scores_of(q, sides_ref[b * half : (b + 1) * half, :HD]) + bias
        parts.append((s, sides_ref[b * half : (b + 1) * half, HD:]))
        top = jnp.maximum(top, jnp.max(s, axis=1, keepdims=True))
    return weighted(parts, top, acc * jnp.exp2(old - top)), top


def mid_kernel(place_ref, q_ref, sides_ref, state_in, state_ref):
    acc, top = far_sum(place_ref, q_ref, sides_ref, state_in)
    state_ref[...] = saved(acc, top)


def last_kernel(place_ref, q_ref, sides_ref, state_in, out_ref):
    acc, top = far_sum(place_ref, q_ref, sides_ref, state_in)
    total = acc[:, HD:]
    out_ref[: QPK * TOK, :] = (acc[:, :HD] / total).astype(jnp.bfloat16)
    level = top + jnp.log2(total)
    level = jnp.concatenate(
        [as_row(level[p * TOK : (p + 1) * TOK]) for p in range(QPK)], axis=0
    )
    high = level.astype(jnp.bfloat16)
    rest = level - high.astype(jnp.float32)
    mid = rest.astype(jnp.bfloat16)
    low = (rest - mid.astype(jnp.float32)).astype(jnp.bfloat16)
    zero = jnp.zeros_like(low)
    out_ref[QPK * TOK :, :] = jnp.concatenate([high, mid, low, zero], axis=0)


def join_kernel(place_ref, a_ref, b_ref, c_ref, d_ref, out_ref):
    head = place_ref[4]
    refs = (a_ref, b_ref, c_ref, d_ref)
    levels = []
    for ref in refs:
        tail = ref[QPK * TOK :, :].astype(jnp.float32)
        levels.append(tail[0:4] + tail[4:8] + tail[8:12])
    top = jnp.maximum(
        jnp.maximum(levels[0], levels[1]), jnp.maximum(levels[2], levels[3])
    )
    shares = [jnp.exp2(level - top) for level in levels]
    total = shares[0] + shares[1] + shares[2] + shares[3]
    shares = [share / total for share in shares]
    for p in range(QPK):
        mixed = jnp.zeros((TOK, HD), jnp.float32)
        for ref, share in zip(refs, shares):
            part = ref[p * TOK : (p + 1) * TOK, :].astype(jnp.float32)
            mixed += as_column(share[p : p + 1]) * part
        mixed = mixed.astype(jnp.bfloat16)
        for quarter in range(4):
            row = pl.multiple_of(lax.rem(quarter + head, 4) * QUARTER, QUARTER)
            out_ref[pl.ds(row, QUARTER), p * HD : (p + 1) * HD] = mixed[
                quarter * QUARTER : (quarter + 1) * QUARTER
            ]


ROWS = QPK * TOK


def whole(a):
    return pl.BlockSpec(a.shape, lambda i, place: (0,) * a.ndim)


def local_call(kernel, steps, in_specs, out_spec, out_shape, operands):
    return pl.pallas_call(
        kernel,
        grid_spec=pltpu.PrefetchScalarGridSpec(
            num_scalar_prefetch=1, grid=(steps,), in_specs=in_specs, out_specs=out_spec
        ),
        out_shape=out_shape,
    )(*operands)


STATE = jax.ShapeDtypeStruct((NX * ROWS, 2 * HD), jnp.float32)


def attend_near(place, q, own, other, frames):
    return local_call(
        near_kernel,
        NX,
        [
            pl.BlockSpec((1, TOK, QPK * HD), lambda i, place: (i, 0, 0)),
            whole(own),
            whole(other),
            whole(frames),
        ],
        pl.BlockSpec((ROWS, 2 * HD), lambda i, place: (i, 0)),
        STATE,
        (place, q, own, other, frames),
    )


def attend_mid(place, q, sides, state):
    return local_call(
        mid_kernel,
        NX,
        [
            pl.BlockSpec((1, TOK, QPK * HD), lambda i, place: (i, 0, 0)),
            whole(sides),
            pl.BlockSpec((ROWS, 2 * HD), lambda i, place: (i, 0)),
        ],
        pl.BlockSpec((ROWS, 2 * HD), lambda i, place: (i, 0)),
        STATE,
        (place, q, sides, state),
    )


def attend_last(place, q, sides, state, slab):
    return local_call(
        last_kernel,
        1,
        [
            pl.BlockSpec((1, TOK, QPK * HD), lambda i, place: (slab, 0, 0)),
            whole(sides),
            pl.BlockSpec((ROWS, 2 * HD), lambda i, place: (slab, 0)),
        ],
        pl.BlockSpec((ROWS + 16, HD), lambda i, place: (0, 0)),
        jax.ShapeDtypeStruct((ROWS + 16, HD), jnp.bfloat16),
        (place, q, sides, state),
    )


def join(place, parts):
    return local_call(
        join_kernel,
        1,
        [whole(part) for part in parts],
        pl.BlockSpec((TOK, QPK * HD), lambda i, place: (0, 0)),
        jax.ShapeDtypeStruct((TOK, QPK * HD), jnp.bfloat16),
        (place, *parts),
    )


def body(patches, merge_index, merge_vals, merger_weight, proj_weight, frame_ids):
    position = lax.axis_index("ctx")
    head = lax.axis_index("head")
    y, z, x, c = split_index(position)
    f32 = jnp.float32

    earlier = jnp.where(y >= FIRST_NY, y - FIRST_NY, y)
    place = jnp.stack([earlier, z, x, c, head]).astype(jnp.int32)
    edge = next_slab(patches[TOK:])
    local = merge_index[0] - (2 * position - 1)
    lower = jnp.where(local[0] == 0, edge, patches[:TOK])
    upper = jnp.where(local[1] == 1, patches[:TOK], patches[TOK:])
    vals = jnp.roll(merge_vals[0], -QUARTER * head, axis=1)
    merged = jnp.dot(vals[0], lower, preferred_element_type=f32) + jnp.dot(
        vals[1], upper, preferred_element_type=f32
    )
    partial = jnp.dot(
        merged.astype(jnp.bfloat16), merger_weight, preferred_element_type=f32
    ).astype(jnp.bfloat16)

    def piece(q, b):
        start = q * QUARTER + b * HALF
        return partial[start : start + HALF]

    up = along_head(jnp.concatenate([piece(2, 0), piece(1, 1)], axis=0), 1)
    down = along_head(jnp.concatenate([piece(2, 1), piece(3, 0)], axis=0), -1)
    up2 = along_head((piece(1, 0).astype(f32) + up[:HALF]).astype(jnp.bfloat16), 1)
    down2 = along_head((piece(3, 1).astype(f32) + down[:HALF]).astype(jnp.bfloat16), -1)
    group = position // (NX * NC)
    octet = lax.dynamic_slice_in_dim(frame_ids, group * (NX * NC * TOK), NX * NC * TOK)
    octet = jnp.roll(octet.reshape(NX * NC, TOK), -QUARTER * head, axis=1)
    octet, place, up2 = lax.optimization_barrier((octet, place, up2))
    first = piece(0, 0).astype(f32) + up2 + down[HALF:]
    second = piece(0, 1).astype(f32) + down2 + up[HALF:]
    hidden = jnp.concatenate([first, second], axis=0)
    mean_square = jnp.mean(hidden * hidden, axis=-1, keepdims=True)
    normed = (hidden * lax.rsqrt(mean_square + 1e-06)).astype(jnp.bfloat16)
    below = along_head(normed, 1)
    above = along_head(normed, -1)
    across_a = along_head(above[:HALF], -1)
    across_b = along_head(below[HALF:], 1)
    normed = jnp.concatenate([normed, above, across_a, across_b, below], axis=0)

    keyvals = jnp.dot(normed, proj_weight[:, QPK * HD :], preferred_element_type=f32)
    keyvals = keyvals.astype(jnp.bfloat16)
    queries = jnp.dot(normed, proj_weight[:, : QPK * HD], preferred_element_type=f32)
    queries = (queries * (LOG2E / math.sqrt(HD))).astype(jnp.bfloat16)

    column = [keyvals]
    for by in range(1, FAR + 1):
        column.append(along_y(keyvals, by))
    column = jnp.concatenate(column, axis=0)
    q_all = [queries]
    for by in range(1, NX):
        q_all.append(along_x(queries, by))
    q_all = jnp.stack(q_all, axis=0)
    column_other = other_core(column)
    sides = []
    for by in (1, 2):
        sides.append(along_z(column, by))
    sides = jnp.concatenate(sides, axis=0)
    sides_other = other_core(sides)

    state = attend_near(place, q_all, column, column_other, octet)
    state = attend_mid(place, q_all, sides, state)
    parts = {}
    for by in (2, 1, 3, 0):
        part = attend_last(place, q_all, sides_other, state, by)
        if by:
            part = along_x(part, -by)
        parts[by] = part
    return join(place, [parts[by] for by in range(NX)])


def solution(mesh):
    return jax.shard_map(
        body,
        mesh=mesh,
        in_specs=(
            P("ctx", "head"),
            P("ctx", None),
            P("ctx", None, None, None),
            P("head", None),
            P(None, "head"),
            P(),
        ),
        out_specs=P("ctx", "head"),
        check_vma=False,
    )
```

profile of v0, /device:TPU:34, one launch (start us, length us, event | category | flops | bytes accessed | tf_op | source)
XLA Modules:
  0.0 217.3 jit_solution(5137251020500632887)
XLA Ops:
  0.0 1.0 slice.69
  1.0 1.9 collective-permute-start
  2.9 0.7 broadcast_subtract_fusion
  3.6 0.6 fusion.28
  4.2 0.9 fusion.24
  6.3 1.2 fusion.14
  7.4 0.2 collective-permute-done
  7.6 3.7 %convolution_convert_fusion = bf16[128,4096]{1,0:T(8,128)(2,1)S(1)} fusion(bf16[640,4096]{1,0:T(8,128)(2,1)} %param.9, f32[128,640]{1,0:T(8,128)S(1)} %fusion.14, bf16[128,640]{1,0:T(8,128)(2,1)S(1)} %collective-permute-done, pred[]{:T(512)} %bitcast.8, bf16[256,640]{1,0:T(8,128)(2,1)} %param.6, bf16[2,128,128]{2,1,0:T(8,128)(2,1)S(1)} %fusion.24), kind=kOutput, calls=%fused_computation | convolution fusion | flops 692830208 | bytes 6980096 | tf_op jit(solution)/shard_map/dot_general | solution.py:294
  11.4 7.9 %collective-permute-start.1 = (bf16[32,4096]{1,0:T(8,128)(2,1)S(1)}, bf16[32,4096]{1,0:T(8,128)(2,1)S(1)}, u32[]{:S(2)}, u32[]{:S(2)}) collective-permute-start(bf16[32,4096]{1,0:T(8,128)(2,1)S(1)} %pad_maximum_fusion.2), channel_id=1, source_target_pairs={{0,1},{1,2},{2,3},{3,0},{4,5},{5,6},{6,7},{7,4},{8,9},{9,10},{10,1... | collective-permute-start | bytes 786440 | tf_op jit(solution)/shard_map/ppermute | solution.py:69
  19.3 8.6 %collective-permute-start.3 = (bf16[32,4096]{1,0:T(8,128)(2,1)S(1)}, bf16[32,4096]{1,0:T(8,128)(2,1)S(1)}, u32[]{:S(2)}, u32[]{:S(2)}) collective-permute-start(bf16[32,4096]{1,0:T(8,128)(2,1)S(1)} %concatenate.34), channel_id=1, source_target_pairs={{0,3},{1,0},{2,1},{3,2},{4,7},{5,4},{6,5},{7,6},{8,11},{9,8},{10,9... | collective-permute-start | bytes 786440 | tf_op jit(solution)/shard_map/ppermute | solution.py:69
  27.9 6.5 %collective-permute-done.1 = bf16[32,4096]{1,0:T(8,128)(2,1)S(1)} collective-permute-done((bf16[32,4096]{1,0:T(8,128)(2,1)S(1)}, bf16[32,4096]{1,0:T(8,128)(2,1)S(1)}, u32[]{:S(2)}, u32[]{:S(2)}) %collective-permute-start.1) | collective-permute-done | bytes 262176 | tf_op jit(solution)/shard_map/ppermute | solution.py:69
  34.5 11.3 %collective-permute-start.2 = (bf16[16,4096]{1,0:T(8,128)(2,1)S(1)}, bf16[16,4096]{1,0:T(8,128)(2,1)S(1)}, u32[]{:S(2)}, u32[]{:S(2)}) collective-permute-start(bf16[16,4096]{1,0:T(8,128)(2,1)S(1)} %add_convert_fusion.1), channel_id=1, source_target_pairs={{0,1},{1,2},{2,3},{3,0},{4,5},{5,6},{6,7},{7,4},{8,9},{9,10},{10,1... | collective-permute-start | bytes 393224 | tf_op jit(solution)/shard_map/ppermute | solution.py:69
  45.9 0.6 stack.38.place_ref
  46.5 0.7 fusion.25.frames_ref
  47.2 10.3 %collective-permute-done.2 = bf16[16,4096]{1,0:T(8,128)(2,1)S(1)} collective-permute-done((bf16[16,4096]{1,0:T(8,128)(2,1)S(1)}, bf16[16,4096]{1,0:T(8,128)(2,1)S(1)}, u32[]{:S(2)}, u32[]{:S(2)}) %collective-permute-start.2) | collective-permute-done | bytes 131104 | tf_op jit(solution)/shard_map/ppermute | solution.py:69
  57.5 0.1 convert_add_fusion.1
  57.5 4.3 %collective-permute-start.4 = (bf16[16,4096]{1,0:T(8,128)(2,1)S(1)}, bf16[16,4096]{1,0:T(8,128)(2,1)S(1)}, u32[]{:S(2)}, u32[]{:S(2)}) collective-permute-start(bf16[16,4096]{1,0:T(8,128)(2,1)S(1)} %get-tuple-element.14), channel_id=1, source_target_pairs={{0,3},{1,0},{2,1},{3,2},{4,7},{5,4},{6,5},{7,6},{8,11},{9,8},{10,9... | collective-permute-start | bytes 393224 | tf_op jit(solution)/shard_map/ppermute | solution.py:69
  61.9 7.9 %collective-permute-done.4 = bf16[16,4096]{1,0:T(8,128)(2,1)S(1)} collective-permute-done((bf16[16,4096]{1,0:T(8,128)(2,1)S(1)}, bf16[16,4096]{1,0:T(8,128)(2,1)S(1)}, u32[]{:S(2)}, u32[]{:S(2)}) %collective-permute-start.4) | collective-permute-done | bytes 131104 | tf_op jit(solution)/shard_map/ppermute | solution.py:69
  69.8 0.2 multiply_reduce_fusion
  70.0 0.1 constant_dynamic-update-slice_fusion.4
  70.1 5.5 %collective-permute-start.5 = (bf16[32,4096]{1,0:T(8,128)(2,1)S(1)}, bf16[32,4096]{1,0:T(8,128)(2,1)S(1)}, u32[]{:S(2)}, u32[]{:S(2)}) collective-permute-start(bf16[32,4096]{1,0:T(8,128)(2,1)S(1)} %get-tuple-element.12), channel_id=1, source_target_pairs={{0,3},{1,0},{2,1},{3,2},{4,7},{5,4},{6,5},{7,6},{8,11},{9,8},{10,9... | collective-permute-start | bytes 786440 | tf_op jit(solution)/shard_map/ppermute | solution.py:69
  75.6 6.7 %collective-permute-start.7 = (bf16[32,4096]{1,0:T(8,128)(2,1)S(1)}, bf16[32,4096]{1,0:T(8,128)(2,1)S(1)}, u32[]{:S(2)}, u32[]{:S(2)}) collective-permute-start(bf16[32,4096]{1,0:T(8,128)(2,1)S(1)} %get-tuple-element.12), channel_id=1, source_target_pairs={{0,1},{1,2},{2,3},{3,0},{4,5},{5,6},{6,7},{7,4},{8,9},{9,10},{10,1... | collective-permute-start | bytes 786440 | tf_op jit(solution)/shard_map/ppermute | solution.py:69
  82.3 7.5 %collective-permute-done.5 = bf16[32,4096]{1,0:T(8,128)(2,1)S(1)} collective-permute-done((bf16[32,4096]{1,0:T(8,128)(2,1)S(1)}, bf16[32,4096]{1,0:T(8,128)(2,1)S(1)}, u32[]{:S(2)}, u32[]{:S(2)}) %collective-permute-start.5) | collective-permute-done | bytes 262176 | tf_op jit(solution)/shard_map/ppermute | solution.py:69
  89.9 3.5 %collective-permute-start.6 = (bf16[16,4096]{1,0:T(8,128)(2,1)S(1)}, bf16[16,4096]{1,0:T(8,128)(2,1)S(1)}, u32[]{:S(2)}, u32[]{:S(2)}) collective-permute-start(bf16[16,4096]{1,0:T(8,128)(2,1)S(1)} %slice.99), channel_id=1, source_target_pairs={{0,3},{1,0},{2,1},{3,2},{4,7},{5,4},{6,5},{7,6},{8,11},{9,8},{10,9... | collective-permute-start | bytes 393224 | tf_op jit(solution)/shard_map/ppermute | solution.py:69
  93.4 4.2 %collective-permute-start.8 = (bf16[16,4096]{1,0:T(8,128)(2,1)S(1)}, bf16[16,4096]{1,0:T(8,128)(2,1)S(1)}, u32[]{:S(2)}, u32[]{:S(2)}) collective-permute-start(bf16[16,4096]{1,0:T(8,128)(2,1)S(1)} %slice.100), channel_id=1, source_target_pairs={{0,1},{1,2},{2,3},{3,0},{4,5},{5,6},{6,7},{7,4},{8,9},{9,10},{10,1... | collective-permute-start | bytes 393224 | tf_op jit(solution)/shard_map/ppermute | solution.py:69
  97.6 1.2 collective-permute-done.6
  98.8 4.5 %collective-permute-done.8 = bf16[16,4096]{1,0:T(8,128)(2,1)S(1)} collective-permute-done((bf16[16,4096]{1,0:T(8,128)(2,1)S(1)}, bf16[16,4096]{1,0:T(8,128)(2,1)S(1)}, u32[]{:S(2)}, u32[]{:S(2)}) %collective-permute-start.8) | collective-permute-done | bytes 131104 | tf_op jit(solution)/shard_map/ppermute | solution.py:69
  103.3 2.1 constant_dynamic-update-slice_fusion.9
  105.4 1.3 collective-permute-start.12
  106.7 1.3 collective-permute-start.13
  108.0 1.3 collective-permute-start.14
  109.3 1.3 collective-permute-start.15
  110.6 2.2 collective-permute-done.12
  112.8 3.0 %collective-permute-done.13 = bf16[128,256]{1,0:T(8,128)(2,1)S(1)} collective-permute-done((bf16[128,256]{1,0:T(8,128)(2,1)S(1)}, bf16[128,256]{1,0:T(8,128)(2,1)S(1)}, u32[]{:S(2)}, u32[]{:S(2)}) %collective-permute-start.13) | collective-permute-done | bytes 65568 | tf_op jit(solution)/shard_map/ppermute | solution.py:37
  115.8 2.8 %collective-permute-done.14 = bf16[128,256]{1,0:T(8,128)(2,1)S(1)} collective-permute-done((bf16[128,256]{1,0:T(8,128)(2,1)S(1)}, bf16[128,256]{1,0:T(8,128)(2,1)S(1)}, u32[]{:S(2)}, u32[]{:S(2)}) %collective-permute-start.14) | collective-permute-done | bytes 65568 | tf_op jit(solution)/shard_map/ppermute | solution.py:37
  118.6 1.9 collective-permute-done.15
  120.5 1.9 collective-permute-start.16
  122.5 4.8 %collective-permute-start.17 = (bf16[640,256]{1,0:T(8,128)(2,1)S(1)}, bf16[640,256]{1,0:T(8,128)(2,1)S(1)}, u32[]{:S(2)}, u32[]{:S(2)}) collective-permute-start(bf16[640,256]{1,0:T(8,128)(2,1)S(1)} %constant_dynamic-update-slice_fusion.5.own_ref), channel_id=1, source_target_pairs={{0,64},{4,68},{8,72},{12,76},{16,80},{20,84},{24,88},{28,92},{32,0... | collective-permute-start | bytes 983048 | tf_op jit(solution)/shard_map/ppermute | solution.py:37
  127.3 1.9 collective-permute-start.19
  129.2 3.9 %collective-permute-done.16 = bf16[640,256]{1,0:T(8,128)(2,1)S(1)} collective-permute-done((bf16[640,256]{1,0:T(8,128)(2,1)S(1)}, bf16[640,256]{1,0:T(8,128)(2,1)S(1)}, u32[]{:S(2)}, u32[]{:S(2)}) %collective-permute-start.16) | collective-permute-done | bytes 327712 | tf_op jit(solution)/shard_map/ppermute | solution.py:37
  133.2 3.3 %collective-permute-done.17 = bf16[640,256]{1,0:T(8,128)(2,1)S(1)} collective-permute-done((bf16[640,256]{1,0:T(8,128)(2,1)S(1)}, bf16[640,256]{1,0:T(8,128)(2,1)S(1)}, u32[]{:S(2)}, u32[]{:S(2)}) %collective-permute-start.17) | collective-permute-done | bytes 327712 | tf_op jit(solution)/shard_map/ppermute | solution.py:37
  136.5 1.9 collective-permute-start.18
  138.5 2.9 %fusion.8 = bf16[128,512]{1,0:T(8,128)(2,1)S(1)} fusion(bf16[128,4096]{1,0:T(8,128)(2,1)S(1)} %constant_dynamic-update-slice_fusion, bf16[4096,768]{1,0:T(8,128)(2,1)} %param.10), kind=kOutput, calls=%fused_computation.8 | convolution fusion | flops 537001984 | bytes 5373952 | tf_op jit(solution)/shard_map/dot_general | solution.py:323
  141.4 3.6 %collective-permute-start.9 = (bf16[128,512]{1,0:T(8,128)(2,1)S(1)}, bf16[128,512]{1,0:T(8,128)(2,1)S(1)}, u32[]{:S(2)}, u32[]{:S(2)}) collective-permute-start(bf16[128,512]{1,0:T(8,128)(2,1)S(1)} %fusion.8), channel_id=1, source_target_pairs={{0,8},{4,12},{8,16},{12,20},{16,24},{20,28},{24,0},{28,4},{32,40},... | collective-permute-start | bytes 393224 | tf_op jit(solution)/shard_map/ppermute | solution.py:37
  145.0 10.5 %collective-permute-start.10 = (bf16[128,512]{1,0:T(8,128)(2,1)S(1)}, bf16[128,512]{1,0:T(8,128)(2,1)S(1)}, u32[]{:S(2)}, u32[]{:S(2)}) collective-permute-start(bf16[128,512]{1,0:T(8,128)(2,1)S(1)} %fusion.8), channel_id=1, source_target_pairs={{0,16},{4,20},{8,24},{12,28},{16,0},{20,4},{24,8},{28,12},{32,48},... | collective-permute-start | bytes 393224 | tf_op jit(solution)/shard_map/ppermute | solution.py:37
  155.5 1.9 collective-permute-start.11
  157.4 2.2 %collective-permute-done.10 = bf16[128,512]{1,0:T(8,128)(2,1)S(1)} collective-permute-done((bf16[128,512]{1,0:T(8,128)(2,1)S(1)}, bf16[128,512]{1,0:T(8,128)(2,1)S(1)}, u32[]{:S(2)}, u32[]{:S(2)}) %collective-permute-start.10) | collective-permute-done | bytes 131104 | tf_op jit(solution)/shard_map/ppermute | solution.py:37
  159.7 3.1 %collective-permute-done.11 = bf16[128,512]{1,0:T(8,128)(2,1)S(1)} collective-permute-done((bf16[128,512]{1,0:T(8,128)(2,1)S(1)}, bf16[128,512]{1,0:T(8,128)(2,1)S(1)}, u32[]{:S(2)}, u32[]{:S(2)}) %collective-permute-start.11) | collective-permute-done | bytes 131104 | tf_op jit(solution)/shard_map/ppermute | solution.py:37
  162.7 0.9 pad_maximum_fusion.1.q_ref
  163.6 0.7 copy-done.3
  164.3 9.0 %shard_map.64.state_in = f32[2048,256]{1,0:T(8,128)} custom-call(s32[5]{0:T(128)} %stack.38.place_ref, bf16[4,128,512]{2,1,0:T(8,128)(2,1)} %pad_maximum_fusion.1.q_ref, bf16[640,256]{1,0:T(8,128)(2,1)} %copy-done.4, bf16[640,256]{1,0:T(8,128)(2,1)} %copy-done.3, s32[8,128]{1,0:T(8,128)} %fusion.25.frames_ref), custom_call_target="tpu_custom_call" | custom-call | tf_op jit(solution)/shard_map/pallas_call | solution.py:209
  173.4 10.0 %shard_map.65.state_in = f32[2048,256]{1,0:T(8,128)} custom-call(s32[5]{0:T(128)} %stack.38.place_ref, bf16[4,128,512]{2,1,0:T(8,128)(2,1)} %pad_maximum_fusion.1.q_ref, bf16[1280,256]{1,0:T(8,128)(2,1)} %copy-done.2, f32[2048,256]{1,0:T(8,128)} %shard_map.64.state_in), custom_call_target="tpu_custom_call" | custom-call | tf_op jit(solution)/shard_map/pallas_call | solution.py:209
  183.4 0.8 copy-done.1
  184.2 4.4 %shard_map.69 = bf16[528,128]{1,0:T(8,128)(2,1)} custom-call(s32[5]{0:T(128)} %stack.38.place_ref, bf16[4,128,512]{2,1,0:T(8,128)(2,1)} %pad_maximum_fusion.1.q_ref, bf16[1280,256]{1,0:T(8,128)(2,1)} %copy-done.1, f32[2048,256]{1,0:T(8,128)} %shard_map.65.state_in), custom_call_target="tpu_custom_call" | custom-call | tf_op jit(solution)/shard_map/pallas_call | solution.py:209
  188.7 1.9 collective-permute-start.22
  190.6 4.4 %shard_map.68 = bf16[528,128]{1,0:T(8,128)(2,1)} custom-call(s32[5]{0:T(128)} %stack.38.place_ref, bf16[4,128,512]{2,1,0:T(8,128)(2,1)} %pad_maximum_fusion.1.q_ref, bf16[1280,256]{1,0:T(8,128)(2,1)} %copy-done.1, f32[2048,256]{1,0:T(8,128)} %shard_map.65.state_in), custom_call_target="tpu_custom_call" | custom-call | tf_op jit(solution)/shard_map/pallas_call | solution.py:209
  195.0 5.3 %collective-permute-start.21 = (bf16[528,128]{1,0:T(8,128)(2,1)}, bf16[528,128]{1,0:T(8,128)(2,1)S(1)}, u32[]{:S(2)}, u32[]{:S(2)}) collective-permute-start(bf16[528,128]{1,0:T(8,128)(2,1)} %shard_map.68), channel_id=1, source_target_pairs={{0,16},{4,20},{8,24},{12,28},{16,0},{20,4},{24,8},{28,12},{32,48},... | collective-permute-start | bytes 405512 | tf_op jit(solution)/shard_map/ppermute | solution.py:37
  200.3 4.4 %shard_map.67 = bf16[528,128]{1,0:T(8,128)(2,1)} custom-call(s32[5]{0:T(128)} %stack.38.place_ref, bf16[4,128,512]{2,1,0:T(8,128)(2,1)} %pad_maximum_fusion.1.q_ref, bf16[1280,256]{1,0:T(8,128)(2,1)} %copy-done.1, f32[2048,256]{1,0:T(8,128)} %shard_map.65.state_in), custom_call_target="tpu_custom_call" | custom-call | tf_op jit(solution)/shard_map/pallas_call | solution.py:209
  204.7 4.0 %collective-permute-start.20 = (bf16[528,128]{1,0:T(8,128)(2,1)}, bf16[528,128]{1,0:T(8,128)(2,1)S(1)}, u32[]{:S(2)}, u32[]{:S(2)}) collective-permute-start(bf16[528,128]{1,0:T(8,128)(2,1)} %shard_map.67), channel_id=1, source_target_pairs={{0,24},{4,28},{8,0},{12,4},{16,8},{20,12},{24,16},{28,20},{32,56},... | collective-permute-start | bytes 405512 | tf_op jit(solution)/shard_map/ppermute | solution.py:37
  208.7 4.4 %shard_map.66.a_ref = bf16[528,128]{1,0:T(8,128)(2,1)} custom-call(s32[5]{0:T(128)} %stack.38.place_ref, bf16[4,128,512]{2,1,0:T(8,128)(2,1)} %pad_maximum_fusion.1.q_ref, bf16[1280,256]{1,0:T(8,128)(2,1)} %copy-done.1, f32[2048,256]{1,0:T(8,128)} %shard_map.65.state_in), custom_call_target="tpu_custom_call" | custom-call | tf_op jit(solution)/shard_map/pallas_call | solution.py:209
  213.1 0.6 copy-done.5
  213.7 0.1 copy-done.6
  213.8 0.6 copy-done.7
  214.4 2.8 %shard_map.70 = bf16[128,512]{1,0:T(8,128)(2,1)} custom-call(s32[5]{0:T(128)} %stack.38.place_ref, bf16[528,128]{1,0:T(8,128)(2,1)} %shard_map.66.a_ref, bf16[528,128]{1,0:T(8,128)(2,1)} %copy-done.7, bf16[528,128]{1,0:T(8,128)(2,1)} %copy-done.6, bf16[528,128]{1,0:T(8,128)(2,1)} %copy-done.5), custom_call_target="tpu_custom_call" | custom-call | tf_op jit(solution)/shard_map/pallas_call | solution.py:209
  (38 shorter events, 0.3 us)
Async XLA Ops:
  0.0 45.8 %copy-start = (s32[24576]{0:T(1024)S(1)}, s32[24576]{0:T(1024)}, u32[]{:S(2)}) copy-start(s32[24576]{0:T(1024)} %param.11) | copy-start | bytes 294916
  1.0 6.6 %collective-permute-start = (bf16[128,640]{1,0:T(8,128)(2,1)S(1)}, bf16[128,640]{1,0:T(8,128)(2,1)S(1)}, u32[]{:S(2)}, u32[]{:S(2)}) collective-permute-start(bf16[128,640]{1,0:T(8,128)(2,1)S(1)} %slice.69), channel_id=1, source_target_pairs={{0,4},{4,8},{8,12},{12,16},{16,20},{20,24},{24,28},{28,32},{32,36}... | collective-permute-start | bytes 491528 | tf_op jit(solution)/shard_map/ppermute | solution.py:65
  11.4 23.1 %collective-permute-start.1 = (bf16[32,4096]{1,0:T(8,128)(2,1)S(1)}, bf16[32,4096]{1,0:T(8,128)(2,1)S(1)}, u32[]{:S(2)}, u32[]{:S(2)}) collective-permute-start(bf16[32,4096]{1,0:T(8,128)(2,1)S(1)} %pad_maximum_fusion.2), channel_id=1, source_target_pairs={{0,1},{1,2},{2,3},{3,0},{4,5},{5,6},{6,7},{7,4},{8,9},{9,10},{10,1... | collective-permute-start | bytes 786440 | tf_op jit(solution)/shard_map/ppermute | solution.py:69
  19.3 38.1 %collective-permute-start.3 = (bf16[32,4096]{1,0:T(8,128)(2,1)S(1)}, bf16[32,4096]{1,0:T(8,128)(2,1)S(1)}, u32[]{:S(2)}, u32[]{:S(2)}) collective-permute-start(bf16[32,4096]{1,0:T(8,128)(2,1)S(1)} %concatenate.34), channel_id=1, source_target_pairs={{0,3},{1,0},{2,1},{3,2},{4,7},{5,4},{6,5},{7,6},{8,11},{9,8},{10,9... | collective-permute-start | bytes 786440 | tf_op jit(solution)/shard_map/ppermute | solution.py:69
  34.5 23.0 %collective-permute-start.2 = (bf16[16,4096]{1,0:T(8,128)(2,1)S(1)}, bf16[16,4096]{1,0:T(8,128)(2,1)S(1)}, u32[]{:S(2)}, u32[]{:S(2)}) collective-permute-start(bf16[16,4096]{1,0:T(8,128)(2,1)S(1)} %add_convert_fusion.1), channel_id=1, source_target_pairs={{0,1},{1,2},{2,3},{3,0},{4,5},{5,6},{6,7},{7,4},{8,9},{9,10},{10,1... | collective-permute-start | bytes 393224 | tf_op jit(solution)/shard_map/ppermute | solution.py:69
  57.5 12.2 %collective-permute-start.4 = (bf16[16,4096]{1,0:T(8,128)(2,1)S(1)}, bf16[16,4096]{1,0:T(8,128)(2,1)S(1)}, u32[]{:S(2)}, u32[]{:S(2)}) collective-permute-start(bf16[16,4096]{1,0:T(8,128)(2,1)S(1)} %get-tuple-element.14), channel_id=1, source_target_pairs={{0,3},{1,0},{2,1},{3,2},{4,7},{5,4},{6,5},{7,6},{8,11},{9,8},{10,9... | collective-permute-start | bytes 393224 | tf_op jit(solution)/shard_map/ppermute | solution.py:69
  70.1 19.8 %collective-permute-start.5 = (bf16[32,4096]{1,0:T(8,128)(2,1)S(1)}, bf16[32,4096]{1,0:T(8,128)(2,1)S(1)}, u32[]{:S(2)}, u32[]{:S(2)}) collective-permute-start(bf16[32,4096]{1,0:T(8,128)(2,1)S(1)} %get-tuple-element.12), channel_id=1, source_target_pairs={{0,3},{1,0},{2,1},{3,2},{4,7},{5,4},{6,5},{7,6},{8,11},{9,8},{10,9... | collective-permute-start | bytes 786440 | tf_op jit(solution)/shard_map/ppermute | solution.py:69
  75.6 17.7 %collective-permute-start.7 = (bf16[32,4096]{1,0:T(8,128)(2,1)S(1)}, bf16[32,4096]{1,0:T(8,128)(2,1)S(1)}, u32[]{:S(2)}, u32[]{:S(2)}) collective-permute-start(bf16[32,4096]{1,0:T(8,128)(2,1)S(1)} %get-tuple-element.12), channel_id=1, source_target_pairs={{0,1},{1,2},{2,3},{3,0},{4,5},{5,6},{6,7},{7,4},{8,9},{9,10},{10,1... | collective-permute-start | bytes 786440 | tf_op jit(solution)/shard_map/ppermute | solution.py:69
  89.9 8.9 %collective-permute-start.6 = (bf16[16,4096]{1,0:T(8,128)(2,1)S(1)}, bf16[16,4096]{1,0:T(8,128)(2,1)S(1)}, u32[]{:S(2)}, u32[]{:S(2)}) collective-permute-start(bf16[16,4096]{1,0:T(8,128)(2,1)S(1)} %slice.99), channel_id=1, source_target_pairs={{0,3},{1,0},{2,1},{3,2},{4,7},{5,4},{6,5},{7,6},{8,11},{9,8},{10,9... | collective-permute-start | bytes 393224 | tf_op jit(solution)/shard_map/ppermute | solution.py:69
  93.4 9.9 %collective-permute-start.8 = (bf16[16,4096]{1,0:T(8,128)(2,1)S(1)}, bf16[16,4096]{1,0:T(8,128)(2,1)S(1)}, u32[]{:S(2)}, u32[]{:S(2)}) collective-permute-start(bf16[16,4096]{1,0:T(8,128)(2,1)S(1)} %slice.100), channel_id=1, source_target_pairs={{0,1},{1,2},{2,3},{3,0},{4,5},{5,6},{6,7},{7,4},{8,9},{9,10},{10,1... | collective-permute-start | bytes 393224 | tf_op jit(solution)/shard_map/ppermute | solution.py:69
  105.4 7.4 %collective-permute-start.12 = (bf16[128,256]{1,0:T(8,128)(2,1)S(1)}, bf16[128,256]{1,0:T(8,128)(2,1)S(1)}, u32[]{:S(2)}, u32[]{:S(2)}) collective-permute-start(bf16[128,256]{1,0:T(8,128)(2,1)S(1)} %get-tuple-element.20), channel_id=1, source_target_pairs={{0,96},{4,100},{8,104},{12,108},{16,112},{20,116},{24,120},{28,124... | collective-permute-start | bytes 196616 | tf_op jit(solution)/shard_map/ppermute | solution.py:37
  106.7 9.1 %collective-permute-start.13 = (bf16[128,256]{1,0:T(8,128)(2,1)S(1)}, bf16[128,256]{1,0:T(8,128)(2,1)S(1)}, u32[]{:S(2)}, u32[]{:S(2)}) collective-permute-start(bf16[128,256]{1,0:T(8,128)(2,1)S(1)} %get-tuple-element.20), channel_id=1, source_target_pairs={{0,192},{4,196},{8,200},{12,204},{16,208},{20,212},{24,216},{28,22... | collective-permute-start | bytes 196616 | tf_op jit(solution)/shard_map/ppermute | solution.py:37
  108.0 10.6 %collective-permute-start.14 = (bf16[128,256]{1,0:T(8,128)(2,1)S(1)}, bf16[128,256]{1,0:T(8,128)(2,1)S(1)}, u32[]{:S(2)}, u32[]{:S(2)}) collective-permute-start(bf16[128,256]{1,0:T(8,128)(2,1)S(1)} %get-tuple-element.20), channel_id=1, source_target_pairs={{0,288},{4,292},{8,296},{12,300},{16,304},{20,308},{24,312},{28,31... | collective-permute-start | bytes 196616 | tf_op jit(solution)/shard_map/ppermute | solution.py:37
  109.3 11.2 %collective-permute-start.15 = (bf16[128,256]{1,0:T(8,128)(2,1)S(1)}, bf16[128,256]{1,0:T(8,128)(2,1)S(1)}, u32[]{:S(2)}, u32[]{:S(2)}) collective-permute-start(bf16[128,256]{1,0:T(8,128)(2,1)S(1)} %get-tuple-element.20), channel_id=1, source_target_pairs={{0,384},{4,388},{8,392},{12,396},{16,400},{20,404},{24,408},{28,41... | collective-permute-start | bytes 196616 | tf_op jit(solution)/shard_map/ppermute | solution.py:37
  120.5 43.1 %copy-start.4 = (bf16[640,256]{1,0:T(8,128)(2,1)}, bf16[640,256]{1,0:T(8,128)(2,1)S(1)}, u32[]{:S(2)}) copy-start(bf16[640,256]{1,0:T(8,128)(2,1)S(1)} %constant_dynamic-update-slice_fusion.5.own_ref) | copy-start | bytes 983044
  120.5 12.6 %collective-permute-start.16 = (bf16[640,256]{1,0:T(8,128)(2,1)S(1)}, bf16[640,256]{1,0:T(8,128)(2,1)S(1)}, u32[]{:S(2)}, u32[]{:S(2)}) collective-permute-start(bf16[640,256]{1,0:T(8,128)(2,1)S(1)} %constant_dynamic-update-slice_fusion.5.own_ref), channel_id=1, source_target_pairs={{0,32},{4,36},{8,40},{12,44},{16,48},{20,52},{24,56},{28,60},{32,6... | collective-permute-start | bytes 983048 | tf_op jit(solution)/shard_map/ppermute | solution.py:37
  122.5 14.0 %collective-permute-start.17 = (bf16[640,256]{1,0:T(8,128)(2,1)S(1)}, bf16[640,256]{1,0:T(8,128)(2,1)S(1)}, u32[]{:S(2)}, u32[]{:S(2)}) collective-permute-start(bf16[640,256]{1,0:T(8,128)(2,1)S(1)} %constant_dynamic-update-slice_fusion.5.own_ref), channel_id=1, source_target_pairs={{0,64},{4,68},{8,72},{12,76},{16,80},{20,84},{24,88},{28,92},{32,0... | collective-permute-start | bytes 983048 | tf_op jit(solution)/shard_map/ppermute | solution.py:37
  127.3 36.3 %collective-permute-start.19 = (bf16[640,256]{1,0:T(8,128)(2,1)S(1)}, bf16[640,256]{1,0:T(8,128)(2,1)S(1)}, u32[]{:S(2)}, u32[]{:S(2)}) collective-permute-start(bf16[640,256]{1,0:T(8,128)(2,1)S(1)} %constant_dynamic-update-slice_fusion.5.own_ref), channel_id=1, source_target_pairs={{0,4},{4,0},{8,12},{12,8},{16,20},{20,16},{24,28},{28,24},{32,36},... | collective-permute-start | bytes 983048 | tf_op jit(solution)/shard_map/ppermute | solution.py:37
  136.5 36.8 %copy-start.2 = (bf16[1280,256]{1,0:T(8,128)(2,1)}, bf16[1280,256]{1,0:T(8,128)(2,1)S(1)}, u32[]{:S(2)}) copy-start(bf16[1280,256]{1,0:T(8,128)(2,1)S(1)} %constant_dynamic-update-slice_fusion.10.sides_ref) | copy-start | bytes 1966084
  136.5 46.9 %collective-permute-start.18 = (bf16[1280,256]{1,0:T(8,128)(2,1)S(1)}, bf16[1280,256]{1,0:T(8,128)(2,1)S(1)}, u32[]{:S(2)}, u32[]{:S(2)}) collective-permute-start(bf16[1280,256]{1,0:T(8,128)(2,1)S(1)} %constant_dynamic-update-slice_fusion.10.sides_ref), channel_id=1, source_target_pairs={{0,4},{4,0},{8,12},{12,8},{16,20},{20,16},{24,28},{28,24},{32,36},... | collective-permute-start | bytes 1966088 | tf_op jit(solution)/shard_map/ppermute | solution.py:37
  141.4 16.0 %collective-permute-start.9 = (bf16[128,512]{1,0:T(8,128)(2,1)S(1)}, bf16[128,512]{1,0:T(8,128)(2,1)S(1)}, u32[]{:S(2)}, u32[]{:S(2)}) collective-permute-start(bf16[128,512]{1,0:T(8,128)(2,1)S(1)} %fusion.8), channel_id=1, source_target_pairs={{0,8},{4,12},{8,16},{12,20},{16,24},{20,28},{24,0},{28,4},{32,40},... | collective-permute-start | bytes 393224 | tf_op jit(solution)/shard_map/ppermute | solution.py:37
  145.0 14.7 %collective-permute-start.10 = (bf16[128,512]{1,0:T(8,128)(2,1)S(1)}, bf16[128,512]{1,0:T(8,128)(2,1)S(1)}, u32[]{:S(2)}, u32[]{:S(2)}) collective-permute-start(bf16[128,512]{1,0:T(8,128)(2,1)S(1)} %fusion.8), channel_id=1, source_target_pairs={{0,16},{4,20},{8,24},{12,28},{16,0},{20,4},{24,8},{28,12},{32,48},... | collective-permute-start | bytes 393224 | tf_op jit(solution)/shard_map/ppermute | solution.py:37
  155.5 7.2 %collective-permute-start.11 = (bf16[128,512]{1,0:T(8,128)(2,1)S(1)}, bf16[128,512]{1,0:T(8,128)(2,1)S(1)}, u32[]{:S(2)}, u32[]{:S(2)}) collective-permute-start(bf16[128,512]{1,0:T(8,128)(2,1)S(1)} %fusion.8), channel_id=1, source_target_pairs={{0,24},{4,28},{8,0},{12,4},{16,8},{20,12},{24,16},{28,20},{32,56},... | collective-permute-start | bytes 393224 | tf_op jit(solution)/shard_map/ppermute | solution.py:37
  163.6 0.7 copy-start.3
  183.4 0.8 copy-start.1
  188.7 24.4 %collective-permute-start.22 = (bf16[528,128]{1,0:T(8,128)(2,1)}, bf16[528,128]{1,0:T(8,128)(2,1)S(1)}, u32[]{:S(2)}, u32[]{:S(2)}) collective-permute-start(bf16[528,128]{1,0:T(8,128)(2,1)} %shard_map.69), channel_id=1, source_target_pairs={{0,8},{4,12},{8,16},{12,20},{16,24},{20,28},{24,0},{28,4},{32,40},... | collective-permute-start | bytes 405512 | tf_op jit(solution)/shard_map/ppermute | solution.py:37
  195.0 18.1 %collective-permute-start.21 = (bf16[528,128]{1,0:T(8,128)(2,1)}, bf16[528,128]{1,0:T(8,128)(2,1)S(1)}, u32[]{:S(2)}, u32[]{:S(2)}) collective-permute-start(bf16[528,128]{1,0:T(8,128)(2,1)} %shard_map.68), channel_id=1, source_target_pairs={{0,16},{4,20},{8,24},{12,28},{16,0},{20,4},{24,8},{28,12},{32,48},... | collective-permute-start | bytes 405512 | tf_op jit(solution)/shard_map/ppermute | solution.py:37
  204.7 8.4 %collective-permute-start.20 = (bf16[528,128]{1,0:T(8,128)(2,1)}, bf16[528,128]{1,0:T(8,128)(2,1)S(1)}, u32[]{:S(2)}, u32[]{:S(2)}) collective-permute-start(bf16[528,128]{1,0:T(8,128)(2,1)} %shard_map.67), channel_id=1, source_target_pairs={{0,24},{4,28},{8,0},{12,4},{16,8},{20,12},{24,16},{28,20},{32,56},... | collective-permute-start | bytes 405512 | tf_op jit(solution)/shard_map/ppermute | solution.py:37
  213.1 0.7 copy-start.5
  213.1 0.7 copy-start.6
  213.8 0.7 copy-start.7
where the time goes:
time: 218 us; the launch traced here: 217 us
  starting transfers between devices  96.8 us (44%)
  waiting for transfers between devices  60.6 us (28%)
  Pallas kernels  39.5 us (18%)
  matrix products  9.86 us (5%)
  local copies, waits for them, and re-layouts  5.24 us (2%)
  other arithmetic  3.55 us (2%)
    ppermute x8, starting transfers between devices, along_head(): return lax.ppermute(shard, 'head', [(i, (i + by) % 4) for i in range(4)])  52 us
    ppermute x14, starting transfers between devices, move(): return lax.ppermute(shard, 'ctx', pairs)  43 us
    pallas_call x7, Pallas kernels, local_call(): pl.pallas_call(kernel, grid_spec=pltpu.PrefetchScalarGridSpec(num_scalar_...  39.5 us
    ppermute x8, waiting for transfers between devices, along_head(): return lax.ppermute(shard, 'head', [(i, (i + by) % 4) for i in range(4)])  37.9 us
    ppermute x14, waiting for transfers between devices, move(): return lax.ppermute(shard, 'ctx', pairs)  22.5 us
  transfers between devices with their start and end apart: 23, of which 15 were waited for; matrix products, arithmetic and copies ran while one was open for 4% of the time, Pallas kernels for 15%

commit v1 on v0

--- a/solution.py
+++ b/solution.py
@@ -1,3 +1,4 @@
+import functools
 import math
 
 import jax
@@ -69,10 +70,6 @@
     return lax.ppermute(shard, "head", [(i, (i + by) % 4) for i in range(4)])
 
 
-def rows_of(q):
-    return jnp.concatenate([q[:, p * HD : (p + 1) * HD] for p in range(QPK)], axis=0)
-
-
 def scores_of(q, keys):
     return lax.dot_general(q, keys, (((1,), (1,)), ((), ())), preferred_element_type=jnp.float32)
 
@@ -100,76 +97,88 @@
     return jnp.concatenate([acc[:, :HD], jnp.where(lane < HD // 2, acc[:, HD:], top)], axis=1)
 
 
-def restored(state_ref):
-    total = jnp.broadcast_to(state_ref[:, HD : HD + 1], (state_ref.shape[0], HD))
-    return jnp.concatenate([state_ref[:, :HD], total], axis=1), state_ref[:, 2 * HD - 1 : 2 * HD]
-
-
-def weighted(parts, top, acc):
-    for s, v in parts:
-        w = jnp.exp2(s - top).astype(jnp.bfloat16)
-        acc += jnp.dot(w, with_ones(v), preferred_element_type=jnp.float32)
-    return acc
+def restored(state):
+    total = jnp.broadcast_to(state[:, HD : HD + 1], (state.shape[0], HD))
+    return jnp.concatenate([state[:, :HD], total], axis=1), state[:, 2 * HD - 1 :]
+
+
+def flash(q, blocks, states):
+    values = [with_ones(v) for _, v, _ in blocks]
+
+    def scores(p):
+        rows = q[:, p * HD : (p + 1) * HD]
+        return [mask(scores_of(rows, keys)) for keys, _, mask in blocks]
+
+    done = []
+    following = scores(0)
+    for p in range(QPK):
+        current = following
+        if p + 1 < QPK:
+            following = scores(p + 1)
+        top = jnp.full((TOK, 1), NEG, jnp.float32) if states is None else states[p][1]
+        for s in current:
+            top = jnp.maximum(top, jnp.max(s, axis=1, keepdims=True))
+        acc = None if states is None else states[p][0] * jnp.exp2(states[p][1] - top)
+        for s, v in zip(current, values):
+            w = jnp.exp2(s - top).astype(jnp.bfloat16)
+            part = jnp.dot(w, v, preferred_element_type=jnp.float32)
+            acc = part if acc is None else acc + part
+        done.append((acc, top))
+    return done
 
 
 def near_kernel(place_ref, q_ref, own_ref, other_ref, frames_ref, state_ref):
     earlier, x, c = place_ref[0], place_ref[2], place_ref[3]
-    q = rows_of(q_ref[0])
     mine = frames_ref[pl.ds(lax.rem(x + NX - pl.program_id(0), NX) * NC + c, 1), :]
     column = as_column(mine.astype(jnp.float32))
-    column = jnp.concatenate([column] * QPK, axis=0)
-    parts = []
+    lane = lax.broadcasted_iota(jnp.int32, (1, FAR * TOK), 1)
+    bias = jnp.where(lane < earlier * TOK, 0.0, NEG)
+    blocks = []
     for ref, row in ((own_ref, x * NC + c), (other_ref, x * NC + 1 - c)):
         frame = frames_ref[pl.ds(row, 1), :].astype(jnp.float32)
-        s = scores_of(q, ref[:TOK, :HD])
-        parts.append((jnp.where(frame <= column, s, NEG), ref[:TOK, HD:]))
-    lane = lax.broadcasted_iota(jnp.int32, (1, FAR * TOK), 1)
-    bias = jnp.where(lane < earlier * TOK, 0.0, NEG)
-    for ref in (own_ref, other_ref):
-        parts.append((scores_of(q, ref[TOK:, :HD]) + bias, ref[TOK:, HD:]))
-    top = jnp.full((ROWS, 1), NEG, jnp.float32)
-    for s, _ in parts:
-        top = jnp.maximum(top, jnp.max(s, axis=1, keepdims=True))
-    acc = weighted(parts, top, jnp.zeros((ROWS, 2 * HD), jnp.float32))
-    state_ref[...] = saved(acc, top)
-
-
-def far_sum(place_ref, q_ref, sides_ref, state_ref):
+        allowed = frame <= column
+        blocks.append(
+            (ref[:TOK, :HD], ref[:TOK, HD:], lambda s, ok=allowed: jnp.where(ok, s, NEG))
+        )
+        blocks.append((ref[TOK:, :HD], ref[TOK:, HD:], lambda s: s + bias))
+    for p, (acc, top) in enumerate(flash(q_ref[0], blocks, None)):
+        state_ref[p * TOK : (p + 1) * TOK, :] = saved(acc, top)
+
+
+def far_kernel(place_ref, q_ref, own_ref, other_ref, state_ref, *out_refs):
     earlier, z = place_ref[0], place_ref[1]
-    q = rows_of(q_ref[0])
     half = (FAR + 1) * TOK
-    acc, old = restored(state_ref)
     lane = lax.broadcasted_iota(jnp.int32, (1, half), 1)
-    parts = []
-    top = old
+    blocks = []
     for b in range(2):
         low = jnp.where(z >= b + 1, 0, TOK)
         bias = jnp.where((lane >= low) & (lane < (earlier + 1) * TOK), 0.0, NEG)
-        s = scores_of(q, sides_ref[b * half : (b + 1) * half, :HD]) + bias
-        parts.append((s, sides_ref[b * half : (b + 1) * half, HD:]))
-        top = jnp.maximum(top, jnp.max(s, axis=1, keepdims=True))
-    return weighted(parts, top, acc * jnp.exp2(old - top)), top
-
-
-def mid_kernel(place_ref, q_ref, sides_ref, state_in, state_ref):
-    acc, top = far_sum(place_ref, q_ref, sides_ref, state_in)
-    state_ref[...] = saved(acc, top)
-
-
-def last_kernel(place_ref, q_ref, sides_ref, state_in, out_ref):
-    acc, top = far_sum(place_ref, q_ref, sides_ref, state_in)
-    total = acc[:, HD:]
-    out_ref[: QPK * TOK, :] = (acc[:, :HD] / total).astype(jnp.bfloat16)
-    level = top + jnp.log2(total)
-    level = jnp.concatenate(
-        [as_row(level[p * TOK : (p + 1) * TOK]) for p in range(QPK)], axis=0
-    )
+        for ref in (own_ref, other_ref):
+            rows = slice(b * half, (b + 1) * half)
+            blocks.append((ref[rows, :HD], ref[rows, HD:], lambda s, e=bias: s + e))
+    states = [restored(state_ref[p * TOK : (p + 1) * TOK, :]) for p in range(QPK)]
+    levels, pieces = [], []
+    for acc, top in flash(q_ref[0], blocks, states):
+        total = acc[:, HD:]
+        pieces.append((acc[:, :HD] / total).astype(jnp.bfloat16))
+        levels.append(as_row(top + jnp.log2(total)))
+    level = jnp.concatenate(levels, axis=0)
     high = level.astype(jnp.bfloat16)
     rest = level - high.astype(jnp.float32)
     mid = rest.astype(jnp.bfloat16)
     low = (rest - mid.astype(jnp.float32)).astype(jnp.bfloat16)
     zero = jnp.zeros_like(low)
-    out_ref[QPK * TOK :, :] = jnp.concatenate([high, mid, low, zero], axis=0)
+    pieces.append(jnp.concatenate([high, mid, low, zero], axis=0))
+
+    def store(out_ref):
+        for p, piece in enumerate(pieces):
+            out_ref[p * TOK : p * TOK + piece.shape[0], :] = piece
+
+    if len(out_refs) == 1:
+        store(out_refs[0])
+    else:
+        for step, out_ref in enumerate(out_refs):
+            pl.when(pl.program_id(0) == step)(functools.partial(store, out_ref))
 
 
 def join_kernel(place_ref, a_ref, b_ref, c_ref, d_ref, out_ref):
@@ -234,33 +243,20 @@
     )
 
 
-def attend_mid(place, q, sides, state):
+def attend_far(place, q, own, other, state, first, steps):
+    part = jax.ShapeDtypeStruct((ROWS + 16, HD), jnp.bfloat16)
     return local_call(
-        mid_kernel,
-        NX,
+        far_kernel,
+        steps,
         [
-            pl.BlockSpec((1, TOK, QPK * HD), lambda i, place: (i, 0, 0)),
-            whole(sides),
-            pl.BlockSpec((ROWS, 2 * HD), lambda i, place: (i, 0)),
+            pl.BlockSpec((1, TOK, QPK * HD), lambda i, place: (first + i, 0, 0)),
+            whole(own),
+            whole(other),
+            pl.BlockSpec((ROWS, 2 * HD), lambda i, place: (first + i, 0)),
         ],
-        pl.BlockSpec((ROWS, 2 * HD), lambda i, place: (i, 0)),
-        STATE,
-        (place, q, sides, state),
-    )
-
-
-def attend_last(place, q, sides, state, slab):
-    return local_call(
-        last_kernel,
-        1,
-        [
-            pl.BlockSpec((1, TOK, QPK * HD), lambda i, place: (slab, 0, 0)),
-            whole(sides),
-            pl.BlockSpec((ROWS, 2 * HD), lambda i, place: (slab, 0)),
-        ],
-        pl.BlockSpec((ROWS + 16, HD), lambda i, place: (0, 0)),
-        jax.ShapeDtypeStruct((ROWS + 16, HD), jnp.bfloat16),
-        (place, q, sides, state),
+        [whole(part)] * steps,
+        [part] * steps,
+        (place, q, own, other, state),
     )
 
 
@@ -299,24 +295,36 @@
         start = q * QUARTER + b * HALF
         return partial[start : start + HALF]
 
-    up = along_head(jnp.concatenate([piece(2, 0), piece(1, 1)], axis=0), 1)
-    down = along_head(jnp.concatenate([piece(2, 1), piece(3, 0)], axis=0), -1)
-    up2 = along_head((piece(1, 0).astype(f32) + up[:HALF]).astype(jnp.bfloat16), 1)
-    down2 = along_head((piece(3, 1).astype(f32) + down[:HALF]).astype(jnp.bfloat16), -1)
+    up_far = along_head(piece(2, 0), 1)
+    down_far = along_head(piece(2, 1), -1)
+    up_near = along_head(piece(1, 1), 1)
+    down_near = along_head(piece(3, 0), -1)
+    up2 = (piece(1, 0).astype(f32) + up_far).astype(jnp.bfloat16)
+    up2 = along_head(up2, 1)
+    down2 = (piece(3, 1).astype(f32) + down_far).astype(jnp.bfloat16)
+    down2 = along_head(down2, -1)
     group = position // (NX * NC)
     octet = lax.dynamic_slice_in_dim(frame_ids, group * (NX * NC * TOK), NX * NC * TOK)
     octet = jnp.roll(octet.reshape(NX * NC, TOK), -QUARTER * head, axis=1)
-    octet, place, up2 = lax.optimization_barrier((octet, place, up2))
-    first = piece(0, 0).astype(f32) + up2 + down[HALF:]
-    second = piece(0, 1).astype(f32) + down2 + up[HALF:]
+    octet, place, up2, down2, up_near, down_near = lax.optimization_barrier(
+        (octet, place, up2, down2, up_near, down_near)
+    )
+    first = piece(0, 0).astype(f32) + up2 + down_near
+    second = piece(0, 1).astype(f32) + down2 + up_near
     hidden = jnp.concatenate([first, second], axis=0)
     mean_square = jnp.mean(hidden * hidden, axis=-1, keepdims=True)
     normed = (hidden * lax.rsqrt(mean_square + 1e-06)).astype(jnp.bfloat16)
-    below = along_head(normed, 1)
-    above = along_head(normed, -1)
-    across_a = along_head(above[:HALF], -1)
-    across_b = along_head(below[HALF:], 1)
-    normed = jnp.concatenate([normed, above, across_a, across_b, below], axis=0)
+    early, late = normed[:HALF], normed[HALF:]
+    above_early = along_head(early, -1)
+    below_late = along_head(late, 1)
+    above_late = along_head(late, -1)
+    below_early = along_head(early, 1)
+    across_early = along_head(above_early, -1)
+    across_late = along_head(below_late, 1)
+    normed = jnp.concatenate(
+        [normed, above_early, above_late, across_early, across_late, below_early, below_late],
+        axis=0,
+    )
 
     keyvals = jnp.dot(normed, proj_weight[:, QPK * HD :], preferred_element_type=f32)
     keyvals = keyvals.astype(jnp.bfloat16)
@@ -339,13 +347,13 @@
     sides_other = other_core(sides)
 
     state = attend_near(place, q_all, column, column_other, octet)
-    state = attend_mid(place, q_all, sides, state)
     parts = {}
-    for by in (2, 1, 3, 0):
-        part = attend_last(place, q_all, sides_other, state, by)
-        if by:
-            part = along_x(part, -by)
-        parts[by] = part
+    for first, steps in ((1, 3), (0, 1)):
+        made = attend_far(place, q_all, sides, sides_other, state, first, steps)
+        for by, part in enumerate(made, first):
+            if by:
+                part = along_x(part, -by)
+            parts[by] = part
     return join(place, [parts[by] for by in range(NX)])
 
 

time: 218 us -> 197 us (0.904)
  the two profiles are of different devices: /device:TPU:34 before, /device:TPU:32 now
where the time goes in v1:
time: 197 us; the launch traced here: 196 us
  starting transfers between devices  104 us (53%)
  waiting for transfers between devices  47.1 us (24%)
  Pallas kernels  25.5 us (13%)
  matrix products  9.87 us (5%)
  local copies, waits for them, and re-layouts  4.66 us (2%)
  other arithmetic  3.49 us (2%)
    ppermute x12, starting transfers between devices, along_head(): return lax.ppermute(shard, 'head', [(i, (i + by) % 4) for i in range(4)])  60.9 us
    ppermute x14, starting transfers between devices, move(): return lax.ppermute(shard, 'ctx', pairs)  41.1 us
    pallas_call x4, Pallas kernels, local_call(): pl.pallas_call(kernel, grid_spec=pltpu.PrefetchScalarGridSpec(num_scalar_...  25.5 us
    ppermute x14, waiting for transfers between devices, move(): return lax.ppermute(shard, 'ctx', pairs)  21.7 us
    ppermute x12, waiting for transfers between devices, along_head(): return lax.ppermute(shard, 'head', [(i, (i + by) % 4) for i in range(4)])  20.2 us
    ppermute x1, waiting for transfers between devices, next_slab(): lax.ppermute(shard, 'ctx', [(i, i + 1) for i in range(count - 1) if i + 1...  5.24 us
  transfers between devices with their start and end apart: 27, of which 15 were waited for; matrix products, arithmetic and copies ran while one was open for 4% of the time, Pallas kernels for 6%

profile of v1, /device:TPU:32, one launch (start us, length us, event | category | flops | bytes accessed | tf_op | source)
XLA Modules:
  0.0 196.3 jit_solution(12285551146484591248)
XLA Ops:
  0.0 1.0 slice.60
  1.0 1.9 collective-permute-start
  2.9 0.7 broadcast_subtract_fusion
  3.6 0.6 fusion.29
  4.2 0.9 fusion.24
  6.3 1.2 fusion.14
  7.5 5.2 %collective-permute-done = bf16[128,640]{1,0:T(8,128)(2,1)S(1)} collective-permute-done((bf16[128,640]{1,0:T(8,128)(2,1)S(1)}, bf16[128,640]{1,0:T(8,128)(2,1)S(1)}, u32[]{:S(2)}, u32[]{:S(2)}) %collective-permute-start) | collective-permute-done | bytes 163872 | tf_op jit(solution)/shard_map/ppermute | solution.py:66
  12.7 3.7 %convolution_convert_fusion = bf16[128,4096]{1,0:T(8,128)(2,1)S(1)} fusion(bf16[640,4096]{1,0:T(8,128)(2,1)} %param.9, f32[128,640]{1,0:T(8,128)S(1)} %fusion.14, bf16[128,640]{1,0:T(8,128)(2,1)S(1)} %collective-permute-done, pred[]{:T(512)} %bitcast.8, bf16[256,640]{1,0:T(8,128)(2,1)} %param.6, bf16[2,128,128]{2,1,0:T(8,128)(2,1)S(1)} %fusion.24), kind=kOutput, calls=%fused_computation | convolution fusion | flops 692830208 | bytes 6980096 | tf_op jit(solution)/shard_map/dot_general | solution.py:290
  16.5 9.1 %collective-permute-start.1 = (bf16[16,4096]{1,0:T(8,128)(2,1)S(1)}, bf16[16,4096]{1,0:T(8,128)(2,1)S(1)}, u32[]{:S(2)}, u32[]{:S(2)}) collective-permute-start(bf16[16,4096]{1,0:T(8,128)(2,1)S(1)} %get-tuple-element.30), channel_id=1, source_target_pairs={{0,1},{1,2},{2,3},{3,0},{4,5},{5,6},{6,7},{7,4},{8,9},{9,10},{10,1... | collective-permute-start | bytes 393224 | tf_op jit(solution)/shard_map/ppermute | solution.py:70
  25.6 7.4 %collective-permute-start.3 = (bf16[16,4096]{1,0:T(8,128)(2,1)S(1)}, bf16[16,4096]{1,0:T(8,128)(2,1)S(1)}, u32[]{:S(2)}, u32[]{:S(2)}) collective-permute-start(bf16[16,4096]{1,0:T(8,128)(2,1)S(1)} %get-tuple-element.29), channel_id=1, source_target_pairs={{0,3},{1,0},{2,1},{3,2},{4,7},{5,4},{6,5},{7,6},{8,11},{9,8},{10,9... | collective-permute-start | bytes 393224 | tf_op jit(solution)/shard_map/ppermute | solution.py:70
  33.0 3.6 %collective-permute-start.5 = (bf16[16,4096]{1,0:T(8,128)(2,1)S(1)}, bf16[16,4096]{1,0:T(8,128)(2,1)S(1)}, u32[]{:S(2)}, u32[]{:S(2)}) collective-permute-start(bf16[16,4096]{1,0:T(8,128)(2,1)S(1)} %get-tuple-element.28), channel_id=1, source_target_pairs={{0,1},{1,2},{2,3},{3,0},{4,5},{5,6},{6,7},{7,4},{8,9},{9,10},{10,1... | collective-permute-start | bytes 393224 | tf_op jit(solution)/shard_map/ppermute | solution.py:70
  36.7 5.2 %collective-permute-start.6 = (bf16[16,4096]{1,0:T(8,128)(2,1)S(1)}, bf16[16,4096]{1,0:T(8,128)(2,1)S(1)}, u32[]{:S(2)}, u32[]{:S(2)}) collective-permute-start(bf16[16,4096]{1,0:T(8,128)(2,1)S(1)} %get-tuple-element.27), channel_id=1, source_target_pairs={{0,3},{1,0},{2,1},{3,2},{4,7},{5,4},{6,5},{7,6},{8,11},{9,8},{10,9... | collective-permute-start | bytes 393224 | tf_op jit(solution)/shard_map/ppermute | solution.py:70
  41.9 0.1 add_convert_fusion
  42.0 6.4 %collective-permute-start.2 = (bf16[16,4096]{1,0:T(8,128)(2,1)S(1)}, bf16[16,4096]{1,0:T(8,128)(2,1)S(1)}, u32[]{:S(2)}, u32[]{:S(2)}) collective-permute-start(bf16[16,4096]{1,0:T(8,128)(2,1)S(1)} %get-tuple-element.32), channel_id=1, source_target_pairs={{0,1},{1,2},{2,3},{3,0},{4,5},{5,6},{6,7},{7,4},{8,9},{9,10},{10,1... | collective-permute-start | bytes 393224 | tf_op jit(solution)/shard_map/ppermute | solution.py:70
  48.3 2.5 %collective-permute-start.4 = (bf16[16,4096]{1,0:T(8,128)(2,1)S(1)}, bf16[16,4096]{1,0:T(8,128)(2,1)S(1)}, u32[]{:S(2)}, u32[]{:S(2)}) collective-permute-start(bf16[16,4096]{1,0:T(8,128)(2,1)S(1)} %get-tuple-element.31), channel_id=1, source_target_pairs={{0,3},{1,0},{2,1},{3,2},{4,7},{5,4},{6,5},{7,6},{8,11},{9,8},{10,9... | collective-permute-start | bytes 393224 | tf_op jit(solution)/shard_map/ppermute | solution.py:70
  50.9 0.7 stack.38.place_ref
  51.6 0.7 fusion.25.frames_ref
  52.3 3.3 %collective-permute-done.2 = bf16[16,4096]{1,0:T(8,128)(2,1)S(1)} collective-permute-done((bf16[16,4096]{1,0:T(8,128)(2,1)S(1)}, bf16[16,4096]{1,0:T(8,128)(2,1)S(1)}, u32[]{:S(2)}, u32[]{:S(2)}) %collective-permute-start.2) | collective-permute-done | bytes 131104 | tf_op jit(solution)/shard_map/ppermute | solution.py:70
  55.5 2.0 %collective-permute-done.4 = bf16[16,4096]{1,0:T(8,128)(2,1)S(1)} collective-permute-done((bf16[16,4096]{1,0:T(8,128)(2,1)S(1)}, bf16[16,4096]{1,0:T(8,128)(2,1)S(1)}, u32[]{:S(2)}, u32[]{:S(2)}) %collective-permute-start.4) | collective-permute-done | bytes 131104 | tf_op jit(solution)/shard_map/ppermute | solution.py:70
  57.6 0.1 convert_add_fusion.1
  57.7 0.2 multiply_reduce_fusion
  57.8 0.1 constant_dynamic-update-slice_fusion.6
  58.0 6.2 %collective-permute-start.7 = (bf16[16,4096]{1,0:T(8,128)(2,1)S(1)}, bf16[16,4096]{1,0:T(8,128)(2,1)S(1)}, u32[]{:S(2)}, u32[]{:S(2)}) collective-permute-start(bf16[16,4096]{1,0:T(8,128)(2,1)S(1)} %get-tuple-element.34), channel_id=1, source_target_pairs={{0,3},{1,0},{2,1},{3,2},{4,7},{5,4},{6,5},{7,6},{8,11},{9,8},{10,9... | collective-permute-start | bytes 393224 | tf_op jit(solution)/shard_map/ppermute | solution.py:70
  64.1 5.1 %collective-permute-start.8 = (bf16[16,4096]{1,0:T(8,128)(2,1)S(1)}, bf16[16,4096]{1,0:T(8,128)(2,1)S(1)}, u32[]{:S(2)}, u32[]{:S(2)}) collective-permute-start(bf16[16,4096]{1,0:T(8,128)(2,1)S(1)} %get-tuple-element.33), channel_id=1, source_target_pairs={{0,3},{1,0},{2,1},{3,2},{4,7},{5,4},{6,5},{7,6},{8,11},{9,8},{10,9... | collective-permute-start | bytes 393224 | tf_op jit(solution)/shard_map/ppermute | solution.py:70
  69.3 2.5 %collective-permute-start.10 = (bf16[16,4096]{1,0:T(8,128)(2,1)S(1)}, bf16[16,4096]{1,0:T(8,128)(2,1)S(1)}, u32[]{:S(2)}, u32[]{:S(2)}) collective-permute-start(bf16[16,4096]{1,0:T(8,128)(2,1)S(1)} %get-tuple-element.33), channel_id=1, source_target_pairs={{0,1},{1,2},{2,3},{3,0},{4,5},{5,6},{6,7},{7,4},{8,9},{9,10},{10,1... | collective-permute-start | bytes 393224 | tf_op jit(solution)/shard_map/ppermute | solution.py:70
  71.8 3.7 %collective-permute-start.12 = (bf16[16,4096]{1,0:T(8,128)(2,1)S(1)}, bf16[16,4096]{1,0:T(8,128)(2,1)S(1)}, u32[]{:S(2)}, u32[]{:S(2)}) collective-permute-start(bf16[16,4096]{1,0:T(8,128)(2,1)S(1)} %get-tuple-element.34), channel_id=1, source_target_pairs={{0,1},{1,2},{2,3},{3,0},{4,5},{5,6},{6,7},{7,4},{8,9},{9,10},{10,1... | collective-permute-start | bytes 393224 | tf_op jit(solution)/shard_map/ppermute | solution.py:70
  75.5 5.2 %collective-permute-start.9 = (bf16[16,4096]{1,0:T(8,128)(2,1)S(1)}, bf16[16,4096]{1,0:T(8,128)(2,1)S(1)}, u32[]{:S(2)}, u32[]{:S(2)}) collective-permute-start(bf16[16,4096]{1,0:T(8,128)(2,1)S(1)} %collective-permute-done.7), channel_id=1, source_target_pairs={{0,3},{1,0},{2,1},{3,2},{4,7},{5,4},{6,5},{7,6},{8,11},{9,8},{10,9... | collective-permute-start | bytes 393224 | tf_op jit(solution)/shard_map/ppermute | solution.py:70
  80.7 6.4 %collective-permute-done.10 = bf16[16,4096]{1,0:T(8,128)(2,1)S(1)} collective-permute-done((bf16[16,4096]{1,0:T(8,128)(2,1)S(1)}, bf16[16,4096]{1,0:T(8,128)(2,1)S(1)}, u32[]{:S(2)}, u32[]{:S(2)}) %collective-permute-start.10) | collective-permute-done | bytes 131104 | tf_op jit(solution)/shard_map/ppermute | solution.py:70
  87.1 4.0 %collective-permute-start.11 = (bf16[16,4096]{1,0:T(8,128)(2,1)S(1)}, bf16[16,4096]{1,0:T(8,128)(2,1)S(1)}, u32[]{:S(2)}, u32[]{:S(2)}) collective-permute-start(bf16[16,4096]{1,0:T(8,128)(2,1)S(1)} %collective-permute-done.10), channel_id=1, source_target_pairs={{0,1},{1,2},{2,3},{3,0},{4,5},{5,6},{6,7},{7,4},{8,9},{9,10},{10,1... | collective-permute-start | bytes 393224 | tf_op jit(solution)/shard_map/ppermute | solution.py:70
  91.1 8.5 %collective-permute-done.11 = bf16[16,4096]{1,0:T(8,128)(2,1)S(1)} collective-permute-done((bf16[16,4096]{1,0:T(8,128)(2,1)S(1)}, bf16[16,4096]{1,0:T(8,128)(2,1)S(1)}, u32[]{:S(2)}, u32[]{:S(2)}) %collective-permute-start.11) | collective-permute-done | bytes 131104 | tf_op jit(solution)/shard_map/ppermute | solution.py:70
  99.7 2.1 %constant_dynamic-update-slice_fusion.11 = (bf16[640,256]{1,0:T(8,128)(2,1)S(1)}, bf16[128,256]{1,0:T(8,128)(2,1)S(1)}) fusion(bf16[128,4096]{1,0:T(8,128)(2,1)S(1)} %constant_dynamic-update-slice_fusion, bf16[4096,768]{1,0:T(8,128)(2,1)} %param.10), kind=kOutput, calls=%fused_computation.41 | convolution fusion | flops 268468224 | bytes 3276800 | tf_op jit(solution)/shard_map/dot_general | solution.py:329
  101.8 1.3 collective-permute-start.16
  103.1 1.3 collective-permute-start.17
  104.4 1.3 collective-permute-start.18
  105.7 1.3 collective-permute-start.19
  107.0 2.2 %collective-permute-done.16 = bf16[128,256]{1,0:T(8,128)(2,1)S(1)} collective-permute-done((bf16[128,256]{1,0:T(8,128)(2,1)S(1)}, bf16[128,256]{1,0:T(8,128)(2,1)S(1)}, u32[]{:S(2)}, u32[]{:S(2)}) %collective-permute-start.16) | collective-permute-done | bytes 65568 | tf_op jit(solution)/shard_map/ppermute | solution.py:38
  109.2 2.2 %collective-permute-done.17 = bf16[128,256]{1,0:T(8,128)(2,1)S(1)} collective-permute-done((bf16[128,256]{1,0:T(8,128)(2,1)S(1)}, bf16[128,256]{1,0:T(8,128)(2,1)S(1)}, u32[]{:S(2)}, u32[]{:S(2)}) %collective-permute-start.17) | collective-permute-done | bytes 65568 | tf_op jit(solution)/shard_map/ppermute | solution.py:38
  111.4 3.4 %collective-permute-done.18 = bf16[128,256]{1,0:T(8,128)(2,1)S(1)} collective-permute-done((bf16[128,256]{1,0:T(8,128)(2,1)S(1)}, bf16[128,256]{1,0:T(8,128)(2,1)S(1)}, u32[]{:S(2)}, u32[]{:S(2)}) %collective-permute-start.18) | collective-permute-done | bytes 65568 | tf_op jit(solution)/shard_map/ppermute | solution.py:38
  114.8 2.2 %collective-permute-done.19 = bf16[128,256]{1,0:T(8,128)(2,1)S(1)} collective-permute-done((bf16[128,256]{1,0:T(8,128)(2,1)S(1)}, bf16[128,256]{1,0:T(8,128)(2,1)S(1)}, u32[]{:S(2)}, u32[]{:S(2)}) %collective-permute-start.19) | collective-permute-done | bytes 65568 | tf_op jit(solution)/shard_map/ppermute | solution.py:38
  117.0 1.9 collective-permute-start.20
  118.9 4.8 %collective-permute-start.21 = (bf16[640,256]{1,0:T(8,128)(2,1)S(1)}, bf16[640,256]{1,0:T(8,128)(2,1)S(1)}, u32[]{:S(2)}, u32[]{:S(2)}) collective-permute-start(bf16[640,256]{1,0:T(8,128)(2,1)S(1)} %constant_dynamic-update-slice_fusion.7.own_ref), channel_id=1, source_target_pairs={{0,64},{4,68},{8,72},{12,76},{16,80},{20,84},{24,88},{28,92},{32,0... | collective-permute-start | bytes 983048 | tf_op jit(solution)/shard_map/ppermute | solution.py:38
  123.7 1.9 collective-permute-start.23
  125.6 3.3 %collective-permute-done.20 = bf16[640,256]{1,0:T(8,128)(2,1)S(1)} collective-permute-done((bf16[640,256]{1,0:T(8,128)(2,1)S(1)}, bf16[640,256]{1,0:T(8,128)(2,1)S(1)}, u32[]{:S(2)}, u32[]{:S(2)}) %collective-permute-start.20) | collective-permute-done | bytes 327712 | tf_op jit(solution)/shard_map/ppermute | solution.py:38
  129.0 3.4 %collective-permute-done.21 = bf16[640,256]{1,0:T(8,128)(2,1)S(1)} collective-permute-done((bf16[640,256]{1,0:T(8,128)(2,1)S(1)}, bf16[640,256]{1,0:T(8,128)(2,1)S(1)}, u32[]{:S(2)}, u32[]{:S(2)}) %collective-permute-start.21) | collective-permute-done | bytes 327712 | tf_op jit(solution)/shard_map/ppermute | solution.py:38
  132.4 1.9 collective-permute-start.22
  134.3 2.9 %fusion.8 = bf16[128,512]{1,0:T(8,128)(2,1)S(1)} fusion(bf16[128,4096]{1,0:T(8,128)(2,1)S(1)} %constant_dynamic-update-slice_fusion, bf16[4096,768]{1,0:T(8,128)(2,1)} %param.10), kind=kOutput, calls=%fused_computation.8 | convolution fusion | flops 537001984 | bytes 5373952 | tf_op jit(solution)/shard_map/dot_general | solution.py:331
  137.3 6.4 %collective-permute-start.13 = (bf16[128,512]{1,0:T(8,128)(2,1)S(1)}, bf16[128,512]{1,0:T(8,128)(2,1)S(1)}, u32[]{:S(2)}, u32[]{:S(2)}) collective-permute-start(bf16[128,512]{1,0:T(8,128)(2,1)S(1)} %fusion.8), channel_id=1, source_target_pairs={{0,8},{4,12},{8,16},{12,20},{16,24},{20,28},{24,0},{28,4},{32,40},... | collective-permute-start | bytes 393224 | tf_op jit(solution)/shard_map/ppermute | solution.py:38
  143.7 4.2 %collective-permute-start.14 = (bf16[128,512]{1,0:T(8,128)(2,1)S(1)}, bf16[128,512]{1,0:T(8,128)(2,1)S(1)}, u32[]{:S(2)}, u32[]{:S(2)}) collective-permute-start(bf16[128,512]{1,0:T(8,128)(2,1)S(1)} %fusion.8), channel_id=1, source_target_pairs={{0,16},{4,20},{8,24},{12,28},{16,0},{20,4},{24,8},{28,12},{32,48},... | collective-permute-start | bytes 393224 | tf_op jit(solution)/shard_map/ppermute | solution.py:38
  147.9 4.5 %collective-permute-start.15 = (bf16[128,512]{1,0:T(8,128)(2,1)S(1)}, bf16[128,512]{1,0:T(8,128)(2,1)S(1)}, u32[]{:S(2)}, u32[]{:S(2)}) collective-permute-start(bf16[128,512]{1,0:T(8,128)(2,1)S(1)} %fusion.8), channel_id=1, source_target_pairs={{0,24},{4,28},{8,0},{12,4},{16,8},{20,12},{24,16},{28,20},{32,56},... | collective-permute-start | bytes 393224 | tf_op jit(solution)/shard_map/ppermute | solution.py:38
  152.5 0.5 collective-permute-done.14
  152.9 2.5 %collective-permute-done.15 = bf16[128,512]{1,0:T(8,128)(2,1)S(1)} collective-permute-done((bf16[128,512]{1,0:T(8,128)(2,1)S(1)}, bf16[128,512]{1,0:T(8,128)(2,1)S(1)}, u32[]{:S(2)}, u32[]{:S(2)}) %collective-permute-start.15) | collective-permute-done | bytes 131104 | tf_op jit(solution)/shard_map/ppermute | solution.py:38
  155.4 0.9 pad_maximum_fusion.1.q_ref
  156.3 0.7 copy-done.3
  157.0 7.5 %shard_map.64.state_ref = f32[2048,256]{1,0:T(8,128)} custom-call(s32[5]{0:T(128)} %stack.38.place_ref, bf16[4,128,512]{2,1,0:T(8,128)(2,1)} %pad_maximum_fusion.1.q_ref, bf16[640,256]{1,0:T(8,128)(2,1)} %copy-done.4, bf16[640,256]{1,0:T(8,128)(2,1)} %copy-done.3, s32[8,128]{1,0:T(8,128)} %fusion.25.frames_ref), custom_call_target="tpu_custom_call" | custom-call | tf_op jit(solution)/shard_map/pallas_call | solution.py:218
  164.5 0.8 copy-done.2
  165.4 10.1 %shard_map.66 = (bf16[528,128]{1,0:T(8,128)(2,1)}, bf16[528,128]{1,0:T(8,128)(2,1)}, bf16[528,128]{1,0:T(8,128)(2,1)}) custom-call(s32[5]{0:T(128)} %stack.38.place_ref, bf16[4,128,512]{2,1,0:T(8,128)(2,1)} %pad_maximum_fusion.1.q_ref, bf16[1280,256]{1,0:T(8,128)(2,1)} %copy-done.1, bf16[1280,256]{1,0:T(8,128)(2,1)} %copy-done.2, ...), custom_call_target="tpu_custom_call" | custom-call | tf_op jit(solution)/shard_map/pallas_call | solution.py:218
  175.4 5.4 %collective-permute-start.24 = (bf16[528,128]{1,0:T(8,128)(2,1)}, bf16[528,128]{1,0:T(8,128)(2,1)S(1)}, u32[]{:S(2)}, u32[]{:S(2)}) collective-permute-start(bf16[528,128]{1,0:T(8,128)(2,1)} %get-tuple-element.20), channel_id=1, source_target_pairs={{0,24},{4,28},{8,0},{12,4},{16,8},{20,12},{24,16},{28,20},{32,56},... | collective-permute-start | bytes 405512 | tf_op jit(solution)/shard_map/ppermute | solution.py:38
  180.9 2.8 %collective-permute-start.25 = (bf16[528,128]{1,0:T(8,128)(2,1)}, bf16[528,128]{1,0:T(8,128)(2,1)S(1)}, u32[]{:S(2)}, u32[]{:S(2)}) collective-permute-start(bf16[528,128]{1,0:T(8,128)(2,1)} %get-tuple-element.21), channel_id=1, source_target_pairs={{0,16},{4,20},{8,24},{12,28},{16,0},{20,4},{24,8},{28,12},{32,48},... | collective-permute-start | bytes 405512 | tf_op jit(solution)/shard_map/ppermute | solution.py:38
  183.7 1.9 collective-permute-start.26
  185.6 5.1 %shard_map.65.a_ref = bf16[528,128]{1,0:T(8,128)(2,1)} custom-call(s32[5]{0:T(128)} %stack.38.place_ref, bf16[4,128,512]{2,1,0:T(8,128)(2,1)} %pad_maximum_fusion.1.q_ref, bf16[1280,256]{1,0:T(8,128)(2,1)} %copy-done.1, bf16[1280,256]{1,0:T(8,128)(2,1)} %copy-done.2, f32[2048,256]{1,0:T(8,128)} %shard_map.64.state_ref), custom_call_target="tpu_custom_call" | custom-call | tf_op jit(solution)/shard_map/pallas_call | solution.py:218
  190.7 0.1 collective-permute-done.25.c_ref
  190.8 2.0 %collective-permute-done.26.d_ref = bf16[528,128]{1,0:T(8,128)(2,1)S(1)} collective-permute-done((bf16[528,128]{1,0:T(8,128)(2,1)}, bf16[528,128]{1,0:T(8,128)(2,1)S(1)}, u32[]{:S(2)}, u32[]{:S(2)}) %collective-permute-start.26) | collective-permute-done | bytes 135200 | tf_op jit(solution)/shard_map/ppermute | solution.py:38
  192.9 0.7 copy-done.7
  193.5 2.8 %shard_map.67 = bf16[128,512]{1,0:T(8,128)(2,1)} custom-call(s32[5]{0:T(128)} %stack.38.place_ref, bf16[528,128]{1,0:T(8,128)(2,1)} %shard_map.65.a_ref, bf16[528,128]{1,0:T(8,128)(2,1)} %copy-done.5, bf16[528,128]{1,0:T(8,128)(2,1)} %copy-done.6, bf16[528,128]{1,0:T(8,128)(2,1)} %copy-done.7), custom_call_target="tpu_custom_call" | custom-call | tf_op jit(solution)/shard_map/pallas_call | solution.py:218
  (41 shorter events, 0.3 us)
Async XLA Ops:
  0.0 50.8 %copy-start = (s32[24576]{0:T(1024)S(1)}, s32[24576]{0:T(1024)}, u32[]{:S(2)}) copy-start(s32[24576]{0:T(1024)} %param.11) | copy-start | bytes 294916
  1.0 11.8 %collective-permute-start = (bf16[128,640]{1,0:T(8,128)(2,1)S(1)}, bf16[128,640]{1,0:T(8,128)(2,1)S(1)}, u32[]{:S(2)}, u32[]{:S(2)}) collective-permute-start(bf16[128,640]{1,0:T(8,128)(2,1)S(1)} %slice.60), channel_id=1, source_target_pairs={{0,4},{4,8},{8,12},{12,16},{16,20},{20,24},{24,28},{28,32},{32,36}... | collective-permute-start | bytes 491528 | tf_op jit(solution)/shard_map/ppermute | solution.py:66
  16.5 25.4 %collective-permute-start.1 = (bf16[16,4096]{1,0:T(8,128)(2,1)S(1)}, bf16[16,4096]{1,0:T(8,128)(2,1)S(1)}, u32[]{:S(2)}, u32[]{:S(2)}) collective-permute-start(bf16[16,4096]{1,0:T(8,128)(2,1)S(1)} %get-tuple-element.30), channel_id=1, source_target_pairs={{0,1},{1,2},{2,3},{3,0},{4,5},{5,6},{6,7},{7,4},{8,9},{9,10},{10,1... | collective-permute-start | bytes 393224 | tf_op jit(solution)/shard_map/ppermute | solution.py:70
  25.6 16.3 %collective-permute-start.3 = (bf16[16,4096]{1,0:T(8,128)(2,1)S(1)}, bf16[16,4096]{1,0:T(8,128)(2,1)S(1)}, u32[]{:S(2)}, u32[]{:S(2)}) collective-permute-start(bf16[16,4096]{1,0:T(8,128)(2,1)S(1)} %get-tuple-element.29), channel_id=1, source_target_pairs={{0,3},{1,0},{2,1},{3,2},{4,7},{5,4},{6,5},{7,6},{8,11},{9,8},{10,9... | collective-permute-start | bytes 393224 | tf_op jit(solution)/shard_map/ppermute | solution.py:70
  33.0 19.3 %collective-permute-start.5 = (bf16[16,4096]{1,0:T(8,128)(2,1)S(1)}, bf16[16,4096]{1,0:T(8,128)(2,1)S(1)}, u32[]{:S(2)}, u32[]{:S(2)}) collective-permute-start(bf16[16,4096]{1,0:T(8,128)(2,1)S(1)} %get-tuple-element.28), channel_id=1, source_target_pairs={{0,1},{1,2},{2,3},{3,0},{4,5},{5,6},{6,7},{7,4},{8,9},{9,10},{10,1... | collective-permute-start | bytes 393224 | tf_op jit(solution)/shard_map/ppermute | solution.py:70
  36.7 15.6 %collective-permute-start.6 = (bf16[16,4096]{1,0:T(8,128)(2,1)S(1)}, bf16[16,4096]{1,0:T(8,128)(2,1)S(1)}, u32[]{:S(2)}, u32[]{:S(2)}) collective-permute-start(bf16[16,4096]{1,0:T(8,128)(2,1)S(1)} %get-tuple-element.27), channel_id=1, source_target_pairs={{0,3},{1,0},{2,1},{3,2},{4,7},{5,4},{6,5},{7,6},{8,11},{9,8},{10,9... | collective-permute-start | bytes 393224 | tf_op jit(solution)/shard_map/ppermute | solution.py:70
  42.0 13.6 %collective-permute-start.2 = (bf16[16,4096]{1,0:T(8,128)(2,1)S(1)}, bf16[16,4096]{1,0:T(8,128)(2,1)S(1)}, u32[]{:S(2)}, u32[]{:S(2)}) collective-permute-start(bf16[16,4096]{1,0:T(8,128)(2,1)S(1)} %get-tuple-element.32), channel_id=1, source_target_pairs={{0,1},{1,2},{2,3},{3,0},{4,5},{5,6},{6,7},{7,4},{8,9},{9,10},{10,1... | collective-permute-start | bytes 393224 | tf_op jit(solution)/shard_map/ppermute | solution.py:70
  48.3 9.2 %collective-permute-start.4 = (bf16[16,4096]{1,0:T(8,128)(2,1)S(1)}, bf16[16,4096]{1,0:T(8,128)(2,1)S(1)}, u32[]{:S(2)}, u32[]{:S(2)}) collective-permute-start(bf16[16,4096]{1,0:T(8,128)(2,1)S(1)} %get-tuple-element.31), channel_id=1, source_target_pairs={{0,3},{1,0},{2,1},{3,2},{4,7},{5,4},{6,5},{7,6},{8,11},{9,8},{10,9... | collective-permute-start | bytes 393224 | tf_op jit(solution)/shard_map/ppermute | solution.py:70
  58.0 17.5 %collective-permute-start.7 = (bf16[16,4096]{1,0:T(8,128)(2,1)S(1)}, bf16[16,4096]{1,0:T(8,128)(2,1)S(1)}, u32[]{:S(2)}, u32[]{:S(2)}) collective-permute-start(bf16[16,4096]{1,0:T(8,128)(2,1)S(1)} %get-tuple-element.34), channel_id=1, source_target_pairs={{0,3},{1,0},{2,1},{3,2},{4,7},{5,4},{6,5},{7,6},{8,11},{9,8},{10,9... | collective-permute-start | bytes 393224 | tf_op jit(solution)/shard_map/ppermute | solution.py:70
  64.1 27.0 %collective-permute-start.8 = (bf16[16,4096]{1,0:T(8,128)(2,1)S(1)}, bf16[16,4096]{1,0:T(8,128)(2,1)S(1)}, u32[]{:S(2)}, u32[]{:S(2)}) collective-permute-start(bf16[16,4096]{1,0:T(8,128)(2,1)S(1)} %get-tuple-element.33), channel_id=1, source_target_pairs={{0,3},{1,0},{2,1},{3,2},{4,7},{5,4},{6,5},{7,6},{8,11},{9,8},{10,9... | collective-permute-start | bytes 393224 | tf_op jit(solution)/shard_map/ppermute | solution.py:70
  69.3 17.8 %collective-permute-start.10 = (bf16[16,4096]{1,0:T(8,128)(2,1)S(1)}, bf16[16,4096]{1,0:T(8,128)(2,1)S(1)}, u32[]{:S(2)}, u32[]{:S(2)}) collective-permute-start(bf16[16,4096]{1,0:T(8,128)(2,1)S(1)} %get-tuple-element.33), channel_id=1, source_target_pairs={{0,1},{1,2},{2,3},{3,0},{4,5},{5,6},{6,7},{7,4},{8,9},{9,10},{10,1... | collective-permute-start | bytes 393224 | tf_op jit(solution)/shard_map/ppermute | solution.py:70
  71.8 27.9 %collective-permute-start.12 = (bf16[16,4096]{1,0:T(8,128)(2,1)S(1)}, bf16[16,4096]{1,0:T(8,128)(2,1)S(1)}, u32[]{:S(2)}, u32[]{:S(2)}) collective-permute-start(bf16[16,4096]{1,0:T(8,128)(2,1)S(1)} %get-tuple-element.34), channel_id=1, source_target_pairs={{0,1},{1,2},{2,3},{3,0},{4,5},{5,6},{6,7},{7,4},{8,9},{9,10},{10,1... | collective-permute-start | bytes 393224 | tf_op jit(solution)/shard_map/ppermute | solution.py:70
  75.5 15.7 %collective-permute-start.9 = (bf16[16,4096]{1,0:T(8,128)(2,1)S(1)}, bf16[16,4096]{1,0:T(8,128)(2,1)S(1)}, u32[]{:S(2)}, u32[]{:S(2)}) collective-permute-start(bf16[16,4096]{1,0:T(8,128)(2,1)S(1)} %collective-permute-done.7), channel_id=1, source_target_pairs={{0,3},{1,0},{2,1},{3,2},{4,7},{5,4},{6,5},{7,6},{8,11},{9,8},{10,9... | collective-permute-start | bytes 393224 | tf_op jit(solution)/shard_map/ppermute | solution.py:70
  87.1 12.6 %collective-permute-start.11 = (bf16[16,4096]{1,0:T(8,128)(2,1)S(1)}, bf16[16,4096]{1,0:T(8,128)(2,1)S(1)}, u32[]{:S(2)}, u32[]{:S(2)}) collective-permute-start(bf16[16,4096]{1,0:T(8,128)(2,1)S(1)} %collective-permute-done.10), channel_id=1, source_target_pairs={{0,1},{1,2},{2,3},{3,0},{4,5},{5,6},{6,7},{7,4},{8,9},{9,10},{10,1... | collective-permute-start | bytes 393224 | tf_op jit(solution)/shard_map/ppermute | solution.py:70
  101.8 7.4 %collective-permute-start.16 = (bf16[128,256]{1,0:T(8,128)(2,1)S(1)}, bf16[128,256]{1,0:T(8,128)(2,1)S(1)}, u32[]{:S(2)}, u32[]{:S(2)}) collective-permute-start(bf16[128,256]{1,0:T(8,128)(2,1)S(1)} %get-tuple-element.38), channel_id=1, source_target_pairs={{0,96},{4,100},{8,104},{12,108},{16,112},{20,116},{24,120},{28,124... | collective-permute-start | bytes 196616 | tf_op jit(solution)/shard_map/ppermute | solution.py:38
  103.1 8.3 %collective-permute-start.17 = (bf16[128,256]{1,0:T(8,128)(2,1)S(1)}, bf16[128,256]{1,0:T(8,128)(2,1)S(1)}, u32[]{:S(2)}, u32[]{:S(2)}) collective-permute-start(bf16[128,256]{1,0:T(8,128)(2,1)S(1)} %get-tuple-element.38), channel_id=1, source_target_pairs={{0,192},{4,196},{8,200},{12,204},{16,208},{20,212},{24,216},{28,22... | collective-permute-start | bytes 196616 | tf_op jit(solution)/shard_map/ppermute | solution.py:38
  104.4 10.3 %collective-permute-start.18 = (bf16[128,256]{1,0:T(8,128)(2,1)S(1)}, bf16[128,256]{1,0:T(8,128)(2,1)S(1)}, u32[]{:S(2)}, u32[]{:S(2)}) collective-permute-start(bf16[128,256]{1,0:T(8,128)(2,1)S(1)} %get-tuple-element.38), channel_id=1, source_target_pairs={{0,288},{4,292},{8,296},{12,300},{16,304},{20,308},{24,312},{28,31... | collective-permute-start | bytes 196616 | tf_op jit(solution)/shard_map/ppermute | solution.py:38
  105.7 11.2 %collective-permute-start.19 = (bf16[128,256]{1,0:T(8,128)(2,1)S(1)}, bf16[128,256]{1,0:T(8,128)(2,1)S(1)}, u32[]{:S(2)}, u32[]{:S(2)}) collective-permute-start(bf16[128,256]{1,0:T(8,128)(2,1)S(1)} %get-tuple-element.38), channel_id=1, source_target_pairs={{0,384},{4,388},{8,392},{12,396},{16,400},{20,404},{24,408},{28,41... | collective-permute-start | bytes 196616 | tf_op jit(solution)/shard_map/ppermute | solution.py:38
  117.0 39.3 %copy-start.4 = (bf16[640,256]{1,0:T(8,128)(2,1)}, bf16[640,256]{1,0:T(8,128)(2,1)S(1)}, u32[]{:S(2)}) copy-start(bf16[640,256]{1,0:T(8,128)(2,1)S(1)} %constant_dynamic-update-slice_fusion.7.own_ref) | copy-start | bytes 983044
  117.0 12.0 %collective-permute-start.20 = (bf16[640,256]{1,0:T(8,128)(2,1)S(1)}, bf16[640,256]{1,0:T(8,128)(2,1)S(1)}, u32[]{:S(2)}, u32[]{:S(2)}) collective-permute-start(bf16[640,256]{1,0:T(8,128)(2,1)S(1)} %constant_dynamic-update-slice_fusion.7.own_ref), channel_id=1, source_target_pairs={{0,32},{4,36},{8,40},{12,44},{16,48},{20,52},{24,56},{28,60},{32,6... | collective-permute-start | bytes 983048 | tf_op jit(solution)/shard_map/ppermute | solution.py:38
  118.9 13.5 %collective-permute-start.21 = (bf16[640,256]{1,0:T(8,128)(2,1)S(1)}, bf16[640,256]{1,0:T(8,128)(2,1)S(1)}, u32[]{:S(2)}, u32[]{:S(2)}) collective-permute-start(bf16[640,256]{1,0:T(8,128)(2,1)S(1)} %constant_dynamic-update-slice_fusion.7.own_ref), channel_id=1, source_target_pairs={{0,64},{4,68},{8,72},{12,76},{16,80},{20,84},{24,88},{28,92},{32,0... | collective-permute-start | bytes 983048 | tf_op jit(solution)/shard_map/ppermute | solution.py:38
  123.7 32.6 %collective-permute-start.23 = (bf16[640,256]{1,0:T(8,128)(2,1)S(1)}, bf16[640,256]{1,0:T(8,128)(2,1)S(1)}, u32[]{:S(2)}, u32[]{:S(2)}) collective-permute-start(bf16[640,256]{1,0:T(8,128)(2,1)S(1)} %constant_dynamic-update-slice_fusion.7.own_ref), channel_id=1, source_target_pairs={{0,4},{4,0},{8,12},{12,8},{16,20},{20,16},{24,28},{28,24},{32,36},... | collective-permute-start | bytes 983048 | tf_op jit(solution)/shard_map/ppermute | solution.py:38
  132.4 32.1 %copy-start.1 = (bf16[1280,256]{1,0:T(8,128)(2,1)}, bf16[1280,256]{1,0:T(8,128)(2,1)S(1)}, u32[]{:S(2)}) copy-start(bf16[1280,256]{1,0:T(8,128)(2,1)S(1)} %constant_dynamic-update-slice_fusion.12.own_ref) | copy-start | bytes 1966084
  132.4 32.1 %collective-permute-start.22 = (bf16[1280,256]{1,0:T(8,128)(2,1)S(1)}, bf16[1280,256]{1,0:T(8,128)(2,1)S(1)}, u32[]{:S(2)}, u32[]{:S(2)}) collective-permute-start(bf16[1280,256]{1,0:T(8,128)(2,1)S(1)} %constant_dynamic-update-slice_fusion.12.own_ref), channel_id=1, source_target_pairs={{0,4},{4,0},{8,12},{12,8},{16,20},{20,16},{24,28},{28,24},{32,36},... | collective-permute-start | bytes 1966088 | tf_op jit(solution)/shard_map/ppermute | solution.py:38
  137.3 15.2 %collective-permute-start.13 = (bf16[128,512]{1,0:T(8,128)(2,1)S(1)}, bf16[128,512]{1,0:T(8,128)(2,1)S(1)}, u32[]{:S(2)}, u32[]{:S(2)}) collective-permute-start(bf16[128,512]{1,0:T(8,128)(2,1)S(1)} %fusion.8), channel_id=1, source_target_pairs={{0,8},{4,12},{8,16},{12,20},{16,24},{20,28},{24,0},{28,4},{32,40},... | collective-permute-start | bytes 393224 | tf_op jit(solution)/shard_map/ppermute | solution.py:38
  143.7 9.3 %collective-permute-start.14 = (bf16[128,512]{1,0:T(8,128)(2,1)S(1)}, bf16[128,512]{1,0:T(8,128)(2,1)S(1)}, u32[]{:S(2)}, u32[]{:S(2)}) collective-permute-start(bf16[128,512]{1,0:T(8,128)(2,1)S(1)} %fusion.8), channel_id=1, source_target_pairs={{0,16},{4,20},{8,24},{12,28},{16,0},{20,4},{24,8},{28,12},{32,48},... | collective-permute-start | bytes 393224 | tf_op jit(solution)/shard_map/ppermute | solution.py:38
  147.9 7.5 %collective-permute-start.15 = (bf16[128,512]{1,0:T(8,128)(2,1)S(1)}, bf16[128,512]{1,0:T(8,128)(2,1)S(1)}, u32[]{:S(2)}, u32[]{:S(2)}) collective-permute-start(bf16[128,512]{1,0:T(8,128)(2,1)S(1)} %fusion.8), channel_id=1, source_target_pairs={{0,24},{4,28},{8,0},{12,4},{16,8},{20,12},{24,16},{28,20},{32,56},... | collective-permute-start | bytes 393224 | tf_op jit(solution)/shard_map/ppermute | solution.py:38
  156.3 0.7 copy-start.3
  164.5 0.8 copy-start.2
  175.4 15.3 %collective-permute-start.24 = (bf16[528,128]{1,0:T(8,128)(2,1)}, bf16[528,128]{1,0:T(8,128)(2,1)S(1)}, u32[]{:S(2)}, u32[]{:S(2)}) collective-permute-start(bf16[528,128]{1,0:T(8,128)(2,1)} %get-tuple-element.20), channel_id=1, source_target_pairs={{0,24},{4,28},{8,0},{12,4},{16,8},{20,12},{24,16},{28,20},{32,56},... | collective-permute-start | bytes 405512 | tf_op jit(solution)/shard_map/ppermute | solution.py:38
  180.9 9.9 %collective-permute-start.25 = (bf16[528,128]{1,0:T(8,128)(2,1)}, bf16[528,128]{1,0:T(8,128)(2,1)S(1)}, u32[]{:S(2)}, u32[]{:S(2)}) collective-permute-start(bf16[528,128]{1,0:T(8,128)(2,1)} %get-tuple-element.21), channel_id=1, source_target_pairs={{0,16},{4,20},{8,24},{12,28},{16,0},{20,4},{24,8},{28,12},{32,48},... | collective-permute-start | bytes 405512 | tf_op jit(solution)/shard_map/ppermute | solution.py:38
  183.7 9.2 %collective-permute-start.26 = (bf16[528,128]{1,0:T(8,128)(2,1)}, bf16[528,128]{1,0:T(8,128)(2,1)S(1)}, u32[]{:S(2)}, u32[]{:S(2)}) collective-permute-start(bf16[528,128]{1,0:T(8,128)(2,1)} %get-tuple-element.22), channel_id=1, source_target_pairs={{0,8},{4,12},{8,16},{12,20},{16,24},{20,28},{24,0},{28,4},{32,40},... | collective-permute-start | bytes 405512 | tf_op jit(solution)/shard_map/ppermute | solution.py:38
  190.7 2.1 %copy-start.5 = (bf16[528,128]{1,0:T(8,128)(2,1)}, bf16[528,128]{1,0:T(8,128)(2,1)S(1)}, u32[]{:S(2)}) copy-start(bf16[528,128]{1,0:T(8,128)(2,1)S(1)} %collective-permute-done.24.b_ref) | copy-start | bytes 405508
  190.8 2.0 %copy-start.6 = (bf16[528,128]{1,0:T(8,128)(2,1)}, bf16[528,128]{1,0:T(8,128)(2,1)S(1)}, u32[]{:S(2)}) copy-start(bf16[528,128]{1,0:T(8,128)(2,1)S(1)} %collective-permute-done.25.c_ref) | copy-start | bytes 405508
  192.9 0.7 copy-start.7
